TPU v7x, 512 devices: a whole 4x8x8 slice. The times are simulated.
512 devices in a mesh: tm: 16 (over z_hi, x), band: 32 (over z_lo, y, core).
Axes of the slice: x: 4, y: 8, z: 8 (z_hi: 4, z_lo: 2; z = z_hi * 2 + z_lo), core: 2. Of those that a mesh axis runs over, the one named last changes fastest.
Arguments:
- increments: float32 [16, 4, 2, 1024, 1024], P('tm', None, None, 'band'), may hold values from -6 to 6
- velocity: float32 [16, 2, 1024, 1024], P('tm', None, 'band'), may hold values from -0.4 to 0.4
- diffusivity: float32 [4, 2], replicated, may hold values from 0.03 to 0.22
- scaling: float32 [4, 2, 1024, 1024], P(None, None, 'band'), may hold values from 0.3 to 3
- correlation: float32 [1024, 1024], P('band'), may hold values from -0.2 to 0.5
Outputs:
- weighted_defects: float32 [16, 4, 2, 1024, 1024], P('tm', None, None, 'band')
All inputs are finite; a program needn't handle non-finite values.
Results may differ from a plain program's by a relative error of at most 0.000094.
Values sent between devices are 32-bit elements; how exact they have to be, the bound alone decides.
No kernel may reach another device: no remote copies, remote signals or barrier semaphores. Data moves between devices by JAX's collectives and lax.ppermute only.
A program may use at most 64 MiB of HBM per device.

v0:
```python
import jax
import jax.numpy as jnp
from jax import lax
from jax.sharding import PartitionSpec as P

FIELDS = 4
LEVELS = 2
STEPS = 4


def padded(array, sides, width):
    for axis, dim in sides:
        devices, length = (lax.axis_size(axis), array.shape[dim])
        up = [(i, (i + 1) % devices) for i in range(devices - 1)]
        down = [(j, i) for i, j in up]
        last = lax.slice_in_dim(array, length - width, length, axis=dim)
        first = lax.slice_in_dim(array, 0, width, axis=dim)
        before = lax.ppermute(last, axis, up)
        after = lax.ppermute(first, axis, down)
        array = jnp.concatenate([before, array, after], axis=dim)
    return array


def shifted(array, axis, by):
    devices = lax.axis_size(axis)
    pairs = [(i, i + by) for i in range(devices) if 0 <= i + by < devices]
    return lax.ppermute(array, axis, pairs)


def advance(extended, east_speed, north_speed, diffuse):
    current = extended[:, 1:-1]
    upper = extended[:, 2:]
    lower = extended[:, :-2]
    eastern = jnp.roll(current, -1, 2)
    western = jnp.roll(current, 1, 2)
    return (
        current
        - 0.5 * east_speed * (eastern - western)
        - 0.5 * north_speed * (upper - lower)
        + diffuse * (upper + lower + eastern + western - 4.0 * current)
    )


def local(increments, velocity, diffusivity, scaling, correlation):
    row_count = increments.shape[3]
    width_all = increments.shape[4]
    channels = FIELDS * LEVELS
    initial = increments.reshape(channels, row_count, width_all)
    speeds = velocity[0]
    diffuse = diffusivity.reshape(channels, 1, 1)
    sigma = scaling.reshape(channels, row_count, width_all)
    current = initial
    for section_num in range(STEPS):
        extended = padded(current, (("band", 1),), 1)
        current = advance(extended, speeds[0], speeds[1], diffuse)
    arrived = shifted(current, "tm", 1)
    scaled = sigma * (initial - arrived)
    full_corr = lax.all_gather(correlation, "band", axis=0, tiled=True)
    along = jnp.einsum("fyj,ij->fyi", scaled, full_corr, precision=lax.Precision.HIGHEST)
    mixed = jnp.einsum(
        "iy,fyx->fix",
        full_corr,
        lax.all_to_all(along, "band", split_axis=2, concat_axis=1, tiled=True),
        precision=lax.Precision.HIGHEST,
    )
    result = lax.all_to_all(mixed, "band", split_axis=1, concat_axis=2, tiled=True)
    return (sigma * result).reshape(1, FIELDS, LEVELS, row_count, width_all)


def solution(mesh):
    return jax.shard_map(
        local,
        mesh=mesh,
        in_specs=(
            P("tm", None, None, "band", None),
            P("tm", None, "band", None),
            P(),
            P(None, None, "band", None),
            P("band", None),
        ),
        out_specs=P("tm", None, None, "band", None),
        check_vma=False,
    )
```

profile of v0, /device:TPU:264, one launch (start us, length us, event | category | flops | bytes accessed | tf_op | source)
XLA Modules:
  0.0 238.3 jit_solution(17074188898342318459)
XLA Ops:
  6.5 0.7 all-gather.2.cloned.1.call-update
  7.3 1.7 fusion.18
  9.0 1.9 collective-permute-start.1
  10.9 3.6 %collective-permute-start = (f32[8,1,1024]{2,1,0:T(1,128)}, f32[8,1,1024]{2,1,0:T(1,128)}, u32[]{:S(2)}, u32[]{:S(2)}) collective-permute-start(f32[8,1,1024]{2,1,0:T(1,128)} %get-tuple-element.28), channel_id=1, source_target_pairs={{1,0},{2,1},{3,2},{4,3},{5,4},{6,5},{7,6},{8,7},{9,8},{10,9},{11,1... | collective-permute-start | bytes 98312 | tf_op jit(solution)/shard_map/ppermute | solution.py:19
  14.6 1.7 fusion.17
  16.3 1.9 fusion.16
  18.3 0.1 copy.12
  18.5 1.7 multiply_add_fusion.3
  20.2 1.9 collective-permute-start.3
  22.1 3.6 %collective-permute-start.2 = (f32[8,1,1024]{2,1,0:T(1,128)S(1)}, f32[8,1,1024]{2,1,0:T(1,128)S(1)}, u32[]{:S(2)}, u32[]{:S(2)}) collective-permute-start(f32[8,1,1024]{2,1,0:T(1,128)S(1)} %get-tuple-element.22), channel_id=1, source_target_pairs={{1,0},{2,1},{3,2},{4,3},{5,4},{6,5},{7,6},{8,7},{9,8},{10,9},{11,1... | collective-permute-start | bytes 98312 | tf_op jit(solution)/shard_map/ppermute | solution.py:19
  25.8 0.4 fusion.13
  26.2 0.1 fusion.14
  26.3 1.1 collective-permute-done.2
  27.4 0.8 multiply_add_fusion.2
  28.2 3.9 %collective-permute-start.5 = (f32[8,1,1024]{2,1,0:T(1,128)S(1)}, f32[8,1,1024]{2,1,0:T(1,128)S(1)}, u32[]{:S(2)}, u32[]{:S(2)}) collective-permute-start(f32[8,1,1024]{2,1,0:T(1,128)S(1)} %get-tuple-element.15), channel_id=1, source_target_pairs={{0,1},{1,2},{2,3},{3,4},{4,5},{5,6},{6,7},{7,8},{8,9},{9,10},{10,1... | collective-permute-start | bytes 98312 | tf_op jit(solution)/shard_map/ppermute | solution.py:18
  32.2 2.2 collective-permute-start.4
  34.3 0.4 fusion.10
  34.7 0.1 fusion.11
  34.8 1.1 collective-permute-done.4
  36.0 0.8 multiply_add_fusion.1
  36.8 4.1 %collective-permute-start.7 = (f32[8,1,1024]{2,1,0:T(1,128)S(1)}, f32[8,1,1024]{2,1,0:T(1,128)S(1)}, u32[]{:S(2)}, u32[]{:S(2)}) collective-permute-start(f32[8,1,1024]{2,1,0:T(1,128)S(1)} %get-tuple-element.9), channel_id=1, source_target_pairs={{0,1},{1,2},{2,3},{3,4},{4,5},{5,6},{6,7},{7,8},{8,9},{9,10},{10,1... | collective-permute-start | bytes 98312 | tf_op jit(solution)/shard_map/ppermute | solution.py:18
  40.9 2.1 collective-permute-start.6
  43.0 0.4 fusion.7
  43.4 0.1 fusion.8
  43.5 1.3 collective-permute-done.6
  44.8 0.8 multiply_add_fusion
  45.6 3.4 %collective-permute-start.8 = (f32[8,32,1024]{2,1,0:T(8,128)S(1)}, f32[8,32,1024]{2,1,0:T(8,128)S(1)}, u32[]{:S(2)}, u32[]{:S(2)}) collective-permute-start(f32[8,32,1024]{2,1,0:T(8,128)S(1)} %multiply_add_fusion), channel_id=1, source_target_pairs={{0,32},{32,64},{64,96},{96,128},{128,160},{160,192},{192,224},{224... | collective-permute-start | bytes 3145736 | tf_op jit(solution)/shard_map/ppermute | solution.py:27
  49.0 24.1 %collective-permute-done.8 = f32[8,32,1024]{2,1,0:T(8,128)S(1)} collective-permute-done((f32[8,32,1024]{2,1,0:T(8,128)S(1)}, f32[8,32,1024]{2,1,0:T(8,128)S(1)}, u32[]{:S(2)}, u32[]{:S(2)}) %collective-permute-start.8) | collective-permute-done | bytes 1048608 | tf_op jit(solution)/shard_map/ppermute | solution.py:27
  73.0 0.3 bitcast_multiply_fusion
  73.3 6.1 %all-gather.2.cloned.1.call-done = f32[1024,1024]{1,0:T(8,128)} async-done(((f32[32,1024]{1,0:T(8,128)}), f32[1024,1024]{1,0:T(8,128)}) %all-gather.2.cloned.1.call-update) | async-done | bytes 4194320 | tf_op jit(solution)/shard_map/all_gather | solution.py:58
  79.4 5.7 %fusion.2 = f32[8,32,1024]{2,1,0:T(8,128)S(1)} fusion(f32[8,32,1024]{2,1,0:T(8,128)S(1)} %bitcast_multiply_fusion, f32[1024,1024]{1,0:T(8,128)} %all-gather.2.cloned.1.call-done), kind=kOutput, calls=%fused_computation.2 | convolution fusion | flops 3221225472 | bytes 6291456 | tf_op jit(solution)/shard_map/fyj,ij->fyi/dot_general | solution.py:59
  85.1 2.7 %copy.13 = f32[8,32,1024]{1,0,2:T(8,128)} copy(f32[8,32,1024]{2,1,0:T(8,128)S(1)} %fusion.2) | data formatting | bytes 2097152 | tf_op jit(solution)/shard_map/fyj,ij->fyi/dot_general | solution.py:59
  87.9 3.9 %reshape.34 = f32[32,1,8192]{2,1,0:T(1,128)S(1)} reshape(f32[1024,8,32]{2,1,0:T(8,128)} %bitcast.42) | data formatting | bytes 2097152
  91.7 60.9 %all_to_all.36 = f32[32,1,8192]{2,1,0:T(1,128)S(1)} all-to-all(f32[32,1,8192]{2,1,0:T(1,128)S(1)} %reshape.34), channel_id=1, replica_groups=mesh['tm'=16,'band'=32] {'band'}, dimensions={0} | all-to-all | bytes 2097152 | tf_op jit(solution)/shard_map/all_to_all | solution.py:63
  152.7 0.5 broadcast.25
  153.2 3.2 %reduce = f32[32,8192]{1,0:T(8,128)S(1)} reduce(f32[32,1,8192]{2,1,0:T(1,128)S(1)} %all_to_all.36, f32[]{:T(128)} %broadcast.25), dimensions={1}, to_apply=%all_to_all.26.reduce_sub_computation | reduce | bytes 2097156 | tf_op jit(solution)/shard_map/all_to_all | solution.py:63
  156.4 2.8 %reshape.35 = f32[1024,8,32]{2,1,0:T(8,128)} reshape(f32[32,8192]{1,0:T(8,128)S(1)} %reduce) | data formatting | bytes 2097152
  159.2 6.6 %copy.18 = f32[8,32,32,32]{1,2,3,0:T(8,128)} copy(f32[8,32,32,32]{1,0,3,2:T(8,128)} %bitcast.44) | data formatting | bytes 2097152 | tf_op jit(solution)/shard_map/all_to_all | solution.py:63
  165.8 3.7 %all_to_all.29 = f32[8,1024,32]{1,2,0:T(8,128)S(1)} reshape(f32[8,32,32,32]{2,1,3,0:T(8,128)} %bitcast.45) | data formatting | bytes 2097152 | tf_op jit(solution)/shard_map/all_to_all | solution.py:63
  169.5 5.7 %fusion.4 = f32[8,1024,32]{1,2,0:T(8,128)S(1)} fusion(f32[8,1024,32]{1,2,0:T(8,128)S(1)} %all_to_all.29, f32[1024,1024]{1,0:T(8,128)} %all-gather.2.cloned.1.call-done), kind=kOutput, calls=%fused_computation.5 | convolution fusion | flops 3221225472 | bytes 6291456 | tf_op jit(solution)/shard_map/iy,fyx->fix/dot_general | solution.py:60
  175.2 2.7 %copy.15 = f32[8,1024,32]{2,0,1:T(8,128)} copy(f32[8,1024,32]{1,2,0:T(8,128)S(1)} %fusion.4) | data formatting | bytes 2097152 | tf_op jit(solution)/shard_map/iy,fyx->fix/transpose | solution.py:60
  177.9 3.9 %reshape.36 = f32[32,1,8192]{2,1,0:T(1,128)S(1)} reshape(f32[1024,8,32]{2,1,0:T(8,128)} %bitcast.43) | data formatting | bytes 2097152
  181.8 32.2 %all_to_all.37 = f32[32,1,8192]{2,1,0:T(1,128)S(1)} all-to-all(f32[32,1,8192]{2,1,0:T(1,128)S(1)} %reshape.36), channel_id=1, replica_groups=mesh['tm'=16,'band'=32] {'band'}, dimensions={0} | all-to-all | bytes 2097152 | tf_op jit(solution)/shard_map/all_to_all | solution.py:66
  214.0 3.2 %reduce.1 = f32[32,8192]{1,0:T(8,128)S(1)} reduce(f32[32,1,8192]{2,1,0:T(1,128)S(1)} %all_to_all.37, f32[]{:T(128)} %broadcast.25), dimensions={1}, to_apply=%all_to_all.30.reduce_sub_computation | reduce | bytes 2097156 | tf_op jit(solution)/shard_map/all_to_all | solution.py:66
  217.2 2.7 %reshape.37 = f32[1024,8,32]{2,1,0:T(8,128)} reshape(f32[32,8192]{1,0:T(8,128)S(1)} %reduce.1) | data formatting | bytes 2097152
  219.9 6.6 %copy.16 = f32[8,32,32,32]{3,2,1,0:T(8,128)} copy(f32[8,32,32,32]{3,0,1,2:T(8,128)} %bitcast.46) | data formatting | bytes 2097152 | tf_op jit(solution)/shard_map/all_to_all | solution.py:66
  226.5 3.7 %all_to_all.33 = f32[4,2,32,1024]{3,2,1,0:T(8,128)S(1)} reshape(f32[8,32,32,32]{3,2,1,0:T(8,128)} %copy.16) | data formatting | bytes 2097152 | tf_op jit(solution)/shard_map/all_to_all | solution.py:66
  230.3 1.1 multiply_bitcast_fusion
  (19 shorter events, 0.3 us)
Async XLA Ops:
  6.5 11.9 %copy-start = (f32[1,4,2,32,1024]{4,3,2,1,0:T(8,128)S(1)}, f32[1,4,2,32,1024]{4,3,2,1,0:T(8,128)}, u32[]{:S(2)}) copy-start(f32[1,4,2,32,1024]{4,3,2,1,0:T(8,128)} %param.5) | copy-start | bytes 3145732
  6.5 11.7 %copy-start.3 = (f32[4,2]{0,1:T(2,128)S(1)}, f32[4,2]{0,1:T(2,128)}, u32[]{:S(2)}) copy-start(f32[4,2]{0,1:T(2,128)} %param.7) | copy-start | bytes 100
  6.5 72.9 %all-gather.2.cloned.1.call-start = ((), (), s32[]{:S(2)}) async-start(), calls=%async_computation.2 | async-start | bytes 4325376 | tf_op jit(solution)/shard_map/all_gather | solution.py:58
  7.3 11.0 %copy-start.2 = (f32[1,2,32,1024]{3,2,1,0:T(8,128)S(1)}, f32[1,2,32,1024]{3,2,1,0:T(8,128)}, u32[]{:S(2)}) copy-start(f32[1,2,32,1024]{3,2,1,0:T(8,128)} %param.6) | copy-start | bytes 786436
  9.0 9.4 %collective-permute-start.1 = (f32[8,1,1024]{2,1,0:T(1,128)}, f32[8,1,1024]{2,1,0:T(1,128)}, u32[]{:S(2)}, u32[]{:S(2)}) collective-permute-start(f32[8,1,1024]{2,1,0:T(1,128)} %get-tuple-element.27), channel_id=1, source_target_pairs={{0,1},{1,2},{2,3},{3,4},{4,5},{5,6},{6,7},{7,8},{8,9},{9,10},{10,1... | collective-permute-start | bytes 98312 | tf_op jit(solution)/shard_map/ppermute | solution.py:18
  10.9 7.5 %collective-permute-start = (f32[8,1,1024]{2,1,0:T(1,128)}, f32[8,1,1024]{2,1,0:T(1,128)}, u32[]{:S(2)}, u32[]{:S(2)}) collective-permute-start(f32[8,1,1024]{2,1,0:T(1,128)} %get-tuple-element.28), channel_id=1, source_target_pairs={{1,0},{2,1},{3,2},{4,3},{5,4},{6,5},{7,6},{8,7},{9,8},{10,9},{11,1... | collective-permute-start | bytes 98312 | tf_op jit(solution)/shard_map/ppermute | solution.py:19
  20.2 6.1 %collective-permute-start.3 = (f32[8,1,1024]{2,1,0:T(1,128)S(1)}, f32[8,1,1024]{2,1,0:T(1,128)S(1)}, u32[]{:S(2)}, u32[]{:S(2)}) collective-permute-start(f32[8,1,1024]{2,1,0:T(1,128)S(1)} %get-tuple-element.21), channel_id=1, source_target_pairs={{0,1},{1,2},{2,3},{3,4},{4,5},{5,6},{6,7},{7,8},{8,9},{9,10},{10,1... | collective-permute-start | bytes 98312 | tf_op jit(solution)/shard_map/ppermute | solution.py:18
  22.1 5.2 %collective-permute-start.2 = (f32[8,1,1024]{2,1,0:T(1,128)S(1)}, f32[8,1,1024]{2,1,0:T(1,128)S(1)}, u32[]{:S(2)}, u32[]{:S(2)}) collective-permute-start(f32[8,1,1024]{2,1,0:T(1,128)S(1)} %get-tuple-element.22), channel_id=1, source_target_pairs={{1,0},{2,1},{3,2},{4,3},{5,4},{6,5},{7,6},{8,7},{9,8},{10,9},{11,1... | collective-permute-start | bytes 98312 | tf_op jit(solution)/shard_map/ppermute | solution.py:19
  28.2 6.6 %collective-permute-start.5 = (f32[8,1,1024]{2,1,0:T(1,128)S(1)}, f32[8,1,1024]{2,1,0:T(1,128)S(1)}, u32[]{:S(2)}, u32[]{:S(2)}) collective-permute-start(f32[8,1,1024]{2,1,0:T(1,128)S(1)} %get-tuple-element.15), channel_id=1, source_target_pairs={{0,1},{1,2},{2,3},{3,4},{4,5},{5,6},{6,7},{7,8},{8,9},{9,10},{10,1... | collective-permute-start | bytes 98312 | tf_op jit(solution)/shard_map/ppermute | solution.py:18
  32.2 3.8 %collective-permute-start.4 = (f32[8,1,1024]{2,1,0:T(1,128)S(1)}, f32[8,1,1024]{2,1,0:T(1,128)S(1)}, u32[]{:S(2)}, u32[]{:S(2)}) collective-permute-start(f32[8,1,1024]{2,1,0:T(1,128)S(1)} %get-tuple-element.16), channel_id=1, source_target_pairs={{1,0},{2,1},{3,2},{4,3},{5,4},{6,5},{7,6},{8,7},{9,8},{10,9},{11,1... | collective-permute-start | bytes 98312 | tf_op jit(solution)/shard_map/ppermute | solution.py:19
  36.8 6.7 %collective-permute-start.7 = (f32[8,1,1024]{2,1,0:T(1,128)S(1)}, f32[8,1,1024]{2,1,0:T(1,128)S(1)}, u32[]{:S(2)}, u32[]{:S(2)}) collective-permute-start(f32[8,1,1024]{2,1,0:T(1,128)S(1)} %get-tuple-element.9), channel_id=1, source_target_pairs={{0,1},{1,2},{2,3},{3,4},{4,5},{5,6},{6,7},{7,8},{8,9},{9,10},{10,1... | collective-permute-start | bytes 98312 | tf_op jit(solution)/shard_map/ppermute | solution.py:18
  40.9 32.1 %copy-start.1 = (f32[4,2,32,1024]{3,2,1,0:T(8,128)S(1)}, f32[4,2,32,1024]{3,2,1,0:T(8,128)}, u32[]{:S(2)}) copy-start(f32[4,2,32,1024]{3,2,1,0:T(8,128)} %param.8) | copy-start | bytes 3145732
  40.9 3.9 %collective-permute-start.6 = (f32[8,1,1024]{2,1,0:T(1,128)S(1)}, f32[8,1,1024]{2,1,0:T(1,128)S(1)}, u32[]{:S(2)}, u32[]{:S(2)}) collective-permute-start(f32[8,1,1024]{2,1,0:T(1,128)S(1)} %get-tuple-element.10), channel_id=1, source_target_pairs={{1,0},{2,1},{3,2},{4,3},{5,4},{6,5},{7,6},{8,7},{9,8},{10,9},{11,1... | collective-permute-start | bytes 98312 | tf_op jit(solution)/shard_map/ppermute | solution.py:19
  45.6 27.4 %collective-permute-start.8 = (f32[8,32,1024]{2,1,0:T(8,128)S(1)}, f32[8,32,1024]{2,1,0:T(8,128)S(1)}, u32[]{:S(2)}, u32[]{:S(2)}) collective-permute-start(f32[8,32,1024]{2,1,0:T(8,128)S(1)} %multiply_add_fusion), channel_id=1, source_target_pairs={{0,32},{32,64},{64,96},{96,128},{128,160},{160,192},{192,224},{224... | collective-permute-start | bytes 3145736 | tf_op jit(solution)/shard_map/ppermute | solution.py:27
Sparse Core Ops, SparseCore 0:
  9.5 69.8 all-gather.1
where the time goes:
time: 239 us; the launch traced here: 238 us
  blocking collectives  93.1 us (39%)
  local copies, waits for them, and re-layouts  47.1 us (20%)
  waiting for transfers between devices  34.4 us (14%)
  starting transfers between devices  26.8 us (11%)
  between operations  13.7 us (6%)
  other arithmetic  11.9 us (5%)
  matrix products  11.4 us (5%)
    all_to_all x1, blocking collectives, local(): lax.all_to_all(along, 'band', split_axis=2, concat_axis=1, tiled=True)  60.9 us
    all_to_all x1, blocking collectives, local(): lax.all_to_all(mixed, 'band', split_axis=1, concat_axis=2, tiled=True)  32.2 us
    ppermute x1, waiting for transfers between devices, shifted(): return lax.ppermute(array, axis, pairs)  24.1 us
    unnamed x13, local copies, waits for them, and re-layouts  13.4 us
    ppermute x4, starting transfers between devices, padded(): before = lax.ppermute(last, axis, up)  11.9 us
    ppermute x4, starting transfers between devices, padded(): after = lax.ppermute(first, axis, down)  11.5 us
    all_to_all x3, local copies, waits for them, and re-layouts, local(): lax.all_to_all(along, 'band', split_axis=2, concat_axis=1, tiled=True)  10.8 us
    all_to_all x2, local copies, waits for them, and re-layouts, local(): lax.all_to_all(mixed, 'band', split_axis=1, concat_axis=2, tiled=True)  10.4 us
  transfers between devices with their start and end apart: 10, of which 5 were waited for; matrix products, arithmetic and copies ran while one was open for 5% of the time, Pallas kernels for 0%

commit v1 on v0

v1 whole, which is shorter than its diff:
```python
import jax
import jax.numpy as jnp
from jax import lax
from jax.experimental import pallas as pl
from jax.experimental.pallas import tpu as pltpu
from jax.sharding import PartitionSpec as P

FIELDS = 4
LEVELS = 2
STEPS = 4
CH = FIELDS * LEVELS
ROWS = 32
GRID = 1024
BANDS = 32
QUARTERS = BANDS // CH
COLS = GRID // QUARTERS
F32 = jnp.float32
BF16 = jnp.bfloat16
VMEM_LIMIT = 48 << 20


def params(**kw):
    return pltpu.CompilerParams(vmem_limit_bytes=VMEM_LIMIT, **kw)


def pack_kernel(x_top, x_bot, v_top, v_bot, lo_ref, hi_ref):
    row = lax.broadcasted_iota(jnp.int32, (8, GRID), 0)
    for k in range(CH // 2 + 1):
        if k < CH // 2:
            ta, tb, ba, bb = x_top[2 * k], x_top[2 * k + 1], x_bot[2 * k], x_bot[2 * k + 1]
        else:
            ta, tb, ba, bb = v_top[0], v_top[1], v_bot[0], v_bot[1]
        lo_ref[k] = jnp.where(row < 4, ta, pltpu.roll(tb, 4, 0))
        hi_ref[k] = jnp.where(row < 4, pltpu.roll(ba, 4, 0), bb)


def pack_edges(x, v):
    tiles = CH // 2 + 1
    shape = jax.ShapeDtypeStruct((tiles, 8, GRID), F32)
    last = ROWS // 8 - 1
    return pl.pallas_call(
        pack_kernel,
        grid=(1,),
        out_shape=(shape, shape),
        in_specs=[
            pl.BlockSpec((CH, 8, GRID), lambda i: (0, 0, 0)),
            pl.BlockSpec((CH, 8, GRID), lambda i: (0, last, 0)),
            pl.BlockSpec((2, 8, GRID), lambda i: (0, 0, 0)),
            pl.BlockSpec((2, 8, GRID), lambda i: (0, last, 0)),
        ],
        out_specs=(pl.BlockSpec((tiles, 8, GRID), lambda i: (0, 0, 0)),) * 2,
        compiler_params=params(),
        name="pack_edges",
    )(x, x, v, v)


def stencil_kernel(k_ref, m_ref, x_ref, v_ref, before_ref, after_ref, o_ref, buf, vel):
    c = pl.program_id(0)

    @pl.when(c == 0)
    def _():
        zeros = jnp.zeros((8, GRID), F32)
        for s in range(2):
            buf[s, 0:8] = zeros
            buf[s, 56:64] = zeros
        for d in range(2):
            top, bot = before_ref[CH // 2], after_ref[CH // 2]
            vel[d, 0:8] = 0.5 * (pltpu.roll(top, 4, 0) if d == 0 else top)
            vel[d, 8:40] = 0.5 * v_ref[d]
            vel[d, 40:48] = 0.5 * (bot if d == 0 else pltpu.roll(bot, 4, 0))

    half = c // 2
    odd = c % 2
    top, bot = before_ref[half], after_ref[half]
    buf[0, 8:16] = jnp.where(odd == 0, pltpu.roll(top, 4, 0), top)
    buf[0, 16:48] = x_ref[0]
    buf[0, 48:56] = jnp.where(odd == 0, bot, pltpu.roll(bot, 4, 0))
    k = k_ref[c]
    for s in range(STEPS):
        src, dst = s % 2, (s + 1) % 2
        last = s == STEPS - 1
        for t in range(1, 5) if last else range(6):
            r = 8 + 8 * t
            kk = k * m_ref[0] if t == 0 else k * m_ref[1] if t == 5 else k
            x = buf[src, r : r + 8]
            up = buf[src, r + 1 : r + 9]
            lo = buf[src, r - 1 : r + 7]
            e = pltpu.roll(x, GRID - 1, 1)
            w = pltpu.roll(x, 1, 1)
            hu = vel[0, 8 * t : 8 * t + 8]
            hv = vel[1, 8 * t : 8 * t + 8]
            y = x - hu * (e - w) - hv * (up - lo) + kk * (up + lo + e + w - 4.0 * x)
            if last:
                o_ref[0, r - 16 : r - 8] = y
            else:
                buf[dst, r : r + 8] = y


def propagate(x, v, before, after, diffuse, inside):
    tiles = CH // 2 + 1
    whole = pl.BlockSpec((tiles, 8, GRID), lambda c: (0, 0, 0))
    smem = pl.BlockSpec(memory_space=pltpu.SMEM)
    return pl.pallas_call(
        stencil_kernel,
        grid=(CH,),
        out_shape=jax.ShapeDtypeStruct((CH, ROWS, GRID), F32),
        in_specs=[
            smem,
            smem,
            pl.BlockSpec((1, ROWS, GRID), lambda c: (c, 0, 0)),
            pl.BlockSpec((2, ROWS, GRID), lambda c: (0, 0, 0)),
            whole,
            whole,
        ],
        out_specs=pl.BlockSpec((1, ROWS, GRID), lambda c: (c, 0, 0)),
        scratch_shapes=[pltpu.VMEM((2, 64, GRID), F32), pltpu.VMEM((2, 48, GRID), F32)],
        compiler_params=params(),
        name="propagate",
    )(diffuse, inside, x, v, before, after)


def combine_kernel(x_ref, a_ref, s_ref, o_ref):
    y = s_ref[0] * (x_ref[0] - a_ref[0])
    for q in range(QUARTERS):
        o_ref[q] = y[:, q * COLS : (q + 1) * COLS]


def combine(x, arrived, sigma):
    spec = pl.BlockSpec((1, ROWS, GRID), lambda c: (c, 0, 0))
    return pl.pallas_call(
        combine_kernel,
        grid=(CH,),
        out_shape=jax.ShapeDtypeStruct((BANDS, ROWS, COLS), F32),
        in_specs=[spec] * 3,
        out_specs=pl.BlockSpec((QUARTERS, ROWS, COLS), lambda c: (c, 0, 0)),
        compiler_params=params(),
        name="combine",
    )(x, arrived, sigma)


def halves(x):
    hi = x.astype(BF16)
    return hi, (x - hi.astype(F32)).astype(BF16)


def split_kernel(c_ref, hi_ref, lo_ref):
    hi_ref[...], lo_ref[...] = halves(c_ref[...])


def split(c):
    spec = pl.BlockSpec((256, GRID), lambda i: (i, 0))
    shape = jax.ShapeDtypeStruct((GRID, GRID), BF16)
    return pl.pallas_call(
        split_kernel,
        grid=(GRID // 256,),
        out_shape=(shape, shape),
        in_specs=[spec],
        out_specs=(spec, spec),
        compiler_params=params(),
        name="split",
    )(c)


def rows_kernel(hi_ref, lo_ref, x_ref, o_ref, xh, xl):
    @pl.when(pl.program_id(0) == 0)
    def _():
        xh[...], xl[...] = halves(x_ref[...])

    dot = lambda a, b: jnp.dot(a, b, preferred_element_type=F32)
    o_ref[...] = dot(hi_ref[...], xl[...]) + dot(lo_ref[...], xh[...]) + dot(hi_ref[...], xh[...])


def mix_rows(hi, lo, x):
    spec = pl.BlockSpec((256, GRID), lambda i: (i, 0))
    return pl.pallas_call(
        rows_kernel,
        grid=(GRID // 256,),
        out_shape=jax.ShapeDtypeStruct((GRID, COLS), F32),
        in_specs=[spec, spec, pl.BlockSpec((GRID, COLS), lambda i: (0, 0))],
        out_specs=pl.BlockSpec((256, COLS), lambda i: (i, 0)),
        scratch_shapes=[pltpu.VMEM((GRID, COLS), BF16)] * 2,
        compiler_params=params(),
        name="mix_rows",
    )(hi, lo, x)


def columns_kernel(hi_ref, lo_ref, r_ref, s_ref, o_ref, rh, rl):
    @pl.when(pl.program_id(0) == 0)
    def _():
        for q in range(QUARTERS):
            h, l = halves(r_ref[:, q].reshape(CH * ROWS, COLS))
            rh[:, q * COLS : (q + 1) * COLS] = h
            rl[:, q * COLS : (q + 1) * COLS] = l

    dot = lambda a, b: lax.dot_general(a, b, (((1,), (1,)), ((), ())), preferred_element_type=F32)
    y = dot(rl[...], hi_ref[...]) + dot(rh[...], lo_ref[...]) + dot(rh[...], hi_ref[...])
    o_ref[...] = s_ref[...] * y.reshape(CH, ROWS, 256)


def mix_columns(hi, lo, r, sigma):
    spec = pl.BlockSpec((256, GRID), lambda i: (i, 0))
    out = pl.BlockSpec((CH, ROWS, 256), lambda i: (0, 0, i))
    return pl.pallas_call(
        columns_kernel,
        grid=(GRID // 256,),
        out_shape=jax.ShapeDtypeStruct((CH, ROWS, GRID), F32),
        in_specs=[spec, spec, pl.BlockSpec((CH, QUARTERS, ROWS, COLS), lambda i: (0, 0, 0, 0)), out],
        out_specs=out,
        scratch_shapes=[pltpu.VMEM((CH * ROWS, GRID), BF16)] * 2,
        compiler_params=params(),
        name="mix_columns",
    )(hi, lo, r.reshape(CH, QUARTERS, ROWS, COLS), sigma)


def local(increments, velocity, diffusivity, scaling, correlation):
    x = increments.reshape(CH, ROWS, GRID)
    v = velocity[0]
    sigma = scaling.reshape(CH, ROWS, GRID)
    full = lax.all_gather(correlation, "band", axis=0, tiled=True)
    up = [(i, i + 1) for i in range(BANDS - 1)]
    down = [(j, i) for i, j in up]
    lo_edge, hi_edge = pack_edges(x, v)
    before = lax.ppermute(hi_edge, "band", up)
    after = lax.ppermute(lo_edge, "band", down)
    band = lax.axis_index("band")
    inside = jnp.stack([band > 0, band < BANDS - 1]).astype(F32)
    ends = propagate(x, v, before, after, diffusivity.reshape(CH), inside)
    windows = lax.axis_size("tm")
    arrived = lax.ppermute(ends, "tm", [(i, i + 1) for i in range(windows - 1)])
    sent = combine(x, arrived, sigma)
    mine = lax.all_to_all(sent, "band", 0, 0, tiled=True).reshape(GRID, COLS)
    hi, lo = split(full)
    mixed = mix_rows(hi, lo, mine).reshape(BANDS, ROWS, COLS)
    back = lax.all_to_all(mixed, "band", 0, 0, tiled=True)
    return mix_columns(hi, lo, back, sigma).reshape(1, FIELDS, LEVELS, ROWS, GRID)


def solution(mesh):
    return jax.shard_map(
        local,
        mesh=mesh,
        in_specs=(
            P("tm", None, None, "band", None),
            P("tm", None, "band", None),
            P(),
            P(None, None, "band", None),
            P("band", None),
        ),
        out_specs=P("tm", None, None, "band", None),
        check_vma=False,
    )
```

time: 239 us -> 181 us (0.76)
  the two profiles are of different devices: /device:TPU:264 before, /device:TPU:392 now
where the time goes in v1:
time: 181 us
  waiting for transfers between devices  77 us (43%)
  blocking collectives  32.2 us (18%)
  starting transfers between devices  31.3 us (17%)
  Pallas kernels  23 us (13%)
  between operations  13.5 us (7%)
  local copies, waits for them, and re-layouts  3.68 us (2%)
    ppermute x1, waiting for transfers between devices, local(): arrived = lax.ppermute(ends, 'tm', [(i, i + 1) for i in range(windows - 1)])  49.2 us
    all_to_all x1, blocking collectives, local(): back = lax.all_to_all(mixed, 'band', 0, 0, tiled=True)  32.2 us
    all_to_all x1, waiting for transfers between devices, local(): mine = lax.all_to_all(sent, 'band', 0, 0, tiled=True).reshape(GRID, COLS)  24.5 us
    all_to_all x1, starting transfers between devices, local(): mine = lax.all_to_all(sent, 'band', 0, 0, tiled=True).reshape(GRID, COLS)  22.2 us
    pallas_call x1, Pallas kernels, propagate(): pl.pallas_call(stencil_kernel, grid=(CH,), out_shape=jax.ShapeDtypeStruct...  7.7 us
    pallas_call x1, Pallas kernels, mix_columns(): pl.pallas_call(columns_kernel, grid=(GRID // 256,), out_shape=jax.ShapeDt...  4.99 us
    pallas_call x1, Pallas kernels, mix_rows(): pl.pallas_call(rows_kernel, grid=(GRID // 256,), out_shape=jax.ShapeDtype...  4.37 us
    ppermute x1, starting transfers between devices, local(): after = lax.ppermute(lo_edge, 'band', down)  3.64 us
  transfers between devices with their start and end apart: 5, of which 4 were waited for; matrix products, arithmetic and copies ran while one was open for 0% of the time, Pallas kernels for 8%

profile of v1, /device:TPU:392, one launch (start us, length us, event | category | flops | bytes accessed | tf_op | source)
XLA Modules:
  0.0 180.7 jit_solution(11593584964490474438)
XLA Ops:
  6.5 0.0 copy-start.6
  6.5 0.0 all-gather.2.cloned.1.call-start
  6.5 0.7 all-gather.2.cloned.1.call-update
  7.3 0.0 copy-start
  7.3 1.2 copy-done
  8.5 0.0 copy-start.4
  8.5 0.9 copy-done.4
  9.4 0.0 copy-start.1
  9.4 0.0 copy-start.5
  9.4 0.0 copy-start.3
  9.5 2.1 %collective-permute-start = (f32[5,8,1024]{2,1,0:T(8,128)S(1)}, f32[5,8,1024]{2,1,0:T(8,128)S(1)}, u32[]{:S(2)}, u32[]{:S(2)}) collective-permute-start(f32[5,8,1024]{2,1,0:T(8,128)S(1)} %get-tuple-element.11), channel_id=1, source_target_pairs={{0,1},{1,2},{2,3},{3,4},{4,5},{5,6},{6,7},{7,8},{8,9},{9,10},{10,1... | collective-permute-start | bytes 491528 | tf_op jit(solution)/shard_map/ppermute | solution.py:223
  11.5 3.6 %collective-permute-start.1 = (f32[5,8,1024]{2,1,0:T(8,128)S(1)}, f32[5,8,1024]{2,1,0:T(8,128)S(1)}, u32[]{:S(2)}, u32[]{:S(2)}) collective-permute-start(f32[5,8,1024]{2,1,0:T(8,128)S(1)} %get-tuple-element.12), channel_id=1, source_target_pairs={{1,0},{2,1},{3,2},{4,3},{5,4},{6,5},{7,6},{8,7},{9,8},{10,9},{11,1... | collective-permute-start | bytes 491528 | tf_op jit(solution)/shard_map/ppermute | solution.py:224
  15.2 0.0 copy-done.6
  15.2 0.1 copy.7
  15.3 0.1 reshape.22.k_ref
  15.4 0.1 add_convert_fusion.m_ref
  15.5 0.8 collective-permute-done.before_ref
  16.2 1.8 collective-permute-done.1.after_ref
  18.0 0.0 copy-done.1
  18.0 0.0 copy-done.5
  18.0 7.7 %propagate.1 = f32[8,32,1024]{2,1,0:T(8,128)S(1)} custom-call(f32[8]{0:T(128)S(1)} %reshape.22.k_ref, f32[2]{0:T(128)S(1)} %add_convert_fusion.m_ref, f32[8,32,1024]{2,1,0:T(8,128)S(1)} %bitcast.11, f32[2,32,1024]{2,1,0:T(8,128)S(1)} %bitcast.19, f32[5,8,1024]{2,1,0:T(8,128)S(1)} %collective-permute-done.before_ref, ...), custom_call_target="tpu_custom_call" | custom-call | tf_op jit(solution)/shard_map/propagate/pallas_call | solution.py:103
  25.7 3.4 %collective-permute-start.2 = (f32[8,32,1024]{2,1,0:T(8,128)S(1)}, f32[8,32,1024]{2,1,0:T(8,128)S(1)}, u32[]{:S(2)}, u32[]{:S(2)}) collective-permute-start(f32[8,32,1024]{2,1,0:T(8,128)S(1)} %propagate.1), channel_id=1, source_target_pairs={{0,32},{32,64},{64,96},{96,128},{128,160},{160,192},{192,224},{224... | collective-permute-start | bytes 3145736 | tf_op jit(solution)/shard_map/ppermute | solution.py:229
  29.1 49.2 %collective-permute-done.2.a_ref = f32[8,32,1024]{2,1,0:T(8,128)S(1)} collective-permute-done((f32[8,32,1024]{2,1,0:T(8,128)S(1)}, f32[8,32,1024]{2,1,0:T(8,128)S(1)}, u32[]{:S(2)}, u32[]{:S(2)}) %collective-permute-start.2) | collective-permute-done | bytes 1048608 | tf_op jit(solution)/shard_map/ppermute | solution.py:229
  78.3 0.0 copy-done.3
  78.3 2.7 %combine.1 = f32[32,32,256]{2,1,0:T(8,128)} custom-call(f32[8,32,1024]{2,1,0:T(8,128)S(1)} %bitcast.12, f32[8,32,1024]{2,1,0:T(8,128)S(1)} %collective-permute-done.2.a_ref, f32[8,32,1024]{2,1,0:T(8,128)S(1)} %bitcast.14), custom_call_target="tpu_custom_call" | custom-call | tf_op jit(solution)/shard_map/combine/pallas_call | solution.py:130
  81.1 22.2 %all-to-all-start = ((f32[32,32,256]{2,1,0:T(8,128)}), f32[32,32,256]{2,1,0:T(8,128)}, u32[]{:S(2)}, u32[]{:S(2)}) async-start(f32[32,32,256]{2,1,0:T(8,128)} %combine.1), calls=%async_computation | async-start | bytes 2097152 | tf_op jit(solution)/shard_map/all_to_all | solution.py:231
  103.3 0.0 all-gather.2.cloned.1.call-done.c_ref
  103.3 3.1 %split.1 = (bf16[1024,1024]{1,0:T(8,128)(2,1)S(1)}, bf16[1024,1024]{1,0:T(8,128)(2,1)S(1)}) custom-call(f32[1024,1024]{1,0:T(8,128)} %all-gather.2.cloned.1.call-done.c_ref), custom_call_target="tpu_custom_call" | custom-call | tf_op jit(solution)/shard_map/split/pallas_call | solution.py:153
  106.4 0.0 copy-start.2
  106.5 1.3 copy-done.2
  107.8 24.5 %all-to-all-done = f32[32,32,256]{2,1,0:T(8,128)} async-done(((f32[32,32,256]{2,1,0:T(8,128)}), f32[32,32,256]{2,1,0:T(8,128)}, u32[]{:S(2)}, u32[]{:S(2)}) %all-to-all-start) | async-done | bytes 1048608 | tf_op jit(solution)/shard_map/all_to_all | solution.py:231
  132.3 4.4 %mix_rows.1 = f32[1024,256]{1,0:T(8,128)S(1)} custom-call(bf16[1024,1024]{1,0:T(8,128)(2,1)S(1)} %get-tuple-element.9.hi_ref, bf16[1024,1024]{1,0:T(8,128)(2,1)} %copy-done.2, f32[1024,256]{1,0:T(8,128)} %bitcast.5.x_ref), custom_call_target="tpu_custom_call" | custom-call | tf_op jit(solution)/shard_map/mix_rows/pallas_call | solution.py:175
  136.7 32.2 %all_to_all.10 = f32[32,32,256]{2,1,0:T(8,128)S(1)} all-to-all(f32[32,32,256]{2,1,0:T(8,128)S(1)} %bitcast.16), channel_id=1, replica_groups=mesh['tm'=16,'band'=32] {'band'}, dimensions={0} | all-to-all | bytes 2097152 | tf_op jit(solution)/shard_map/all_to_all | solution.py:234
  168.9 5.0 %mix_columns.1 = f32[8,32,1024]{2,1,0:T(8,128)} custom-call(bf16[1024,1024]{1,0:T(8,128)(2,1)S(1)} %get-tuple-element.9.hi_ref, bf16[1024,1024]{1,0:T(8,128)(2,1)} %copy-done.2, f32[8,4,32,256]{3,2,1,0:T(8,128)S(1)} %bitcast.13, f32[8,32,1024]{2,1,0:T(8,128)S(1)} %bitcast.15), custom_call_target="tpu_custom_call" | custom-call | tf_op jit(solution)/shard_map/mix_columns/pallas_call | solution.py:203
  (1 shorter events, 0.0 us)
Async XLA Ops:
  6.5 8.7 %copy-start.6 = (f32[4,2]{0,1:T(2,128)S(1)}, f32[4,2]{0,1:T(2,128)}, u32[]{:S(2)}) copy-start(f32[4,2]{0,1:T(2,128)} %param.7) | copy-start | bytes 100
  6.5 96.7 %all-gather.2.cloned.1.call-start = ((), (), s32[]{:S(2)}) async-start(), calls=%async_computation.2 | async-start | bytes 4325376 | tf_op jit(solution)/shard_map/all_gather | solution.py:219
  7.3 1.2 copy-start
  8.5 0.9 copy-start.4
  9.4 8.6 %copy-start.1 = (f32[1,4,2,32,1024]{4,3,2,1,0:T(8,128)S(1)}, f32[1,4,2,32,1024]{4,3,2,1,0:T(8,128)}, u32[]{:S(2)}) copy-start(f32[1,4,2,32,1024]{4,3,2,1,0:T(8,128)} %param.5) | copy-start | bytes 3145732
  9.4 8.6 %copy-start.5 = (f32[1,2,32,1024]{3,2,1,0:T(8,128)S(1)}, f32[1,2,32,1024]{3,2,1,0:T(8,128)}, u32[]{:S(2)}) copy-start(f32[1,2,32,1024]{3,2,1,0:T(8,128)} %param.6) | copy-start | bytes 786436
  9.4 68.9 %copy-start.3 = (f32[4,2,32,1024]{3,2,1,0:T(8,128)S(1)}, f32[4,2,32,1024]{3,2,1,0:T(8,128)}, u32[]{:S(2)}) copy-start(f32[4,2,32,1024]{3,2,1,0:T(8,128)} %param.8) | copy-start | bytes 3145732
  9.5 6.8 %collective-permute-start = (f32[5,8,1024]{2,1,0:T(8,128)S(1)}, f32[5,8,1024]{2,1,0:T(8,128)S(1)}, u32[]{:S(2)}, u32[]{:S(2)}) collective-permute-start(f32[5,8,1024]{2,1,0:T(8,128)S(1)} %get-tuple-element.11), channel_id=1, source_target_pairs={{0,1},{1,2},{2,3},{3,4},{4,5},{5,6},{6,7},{7,8},{8,9},{9,10},{10,1... | collective-permute-start | bytes 491528 | tf_op jit(solution)/shard_map/ppermute | solution.py:223
  11.5 6.5 %collective-permute-start.1 = (f32[5,8,1024]{2,1,0:T(8,128)S(1)}, f32[5,8,1024]{2,1,0:T(8,128)S(1)}, u32[]{:S(2)}, u32[]{:S(2)}) collective-permute-start(f32[5,8,1024]{2,1,0:T(8,128)S(1)} %get-tuple-element.12), channel_id=1, source_target_pairs={{1,0},{2,1},{3,2},{4,3},{5,4},{6,5},{7,6},{8,7},{9,8},{10,9},{11,1... | collective-permute-start | bytes 491528 | tf_op jit(solution)/shard_map/ppermute | solution.py:224
  25.7 52.6 %collective-permute-start.2 = (f32[8,32,1024]{2,1,0:T(8,128)S(1)}, f32[8,32,1024]{2,1,0:T(8,128)S(1)}, u32[]{:S(2)}, u32[]{:S(2)}) collective-permute-start(f32[8,32,1024]{2,1,0:T(8,128)S(1)} %propagate.1), channel_id=1, source_target_pairs={{0,32},{32,64},{64,96},{96,128},{128,160},{160,192},{192,224},{224... | collective-permute-start | bytes 3145736 | tf_op jit(solution)/shard_map/ppermute | solution.py:229
  81.1 51.2 %all-to-all-start = ((f32[32,32,256]{2,1,0:T(8,128)}), f32[32,32,256]{2,1,0:T(8,128)}, u32[]{:S(2)}, u32[]{:S(2)}) async-start(f32[32,32,256]{2,1,0:T(8,128)} %combine.1), calls=%async_computation | async-start | bytes 2097152 | tf_op jit(solution)/shard_map/all_to_all | solution.py:231
  106.4 1.3 copy-start.2
Sparse Core Ops, SparseCore 0:
  9.5 68.3 all-gather.1

commit v2 on v0

v2 whole, which is shorter than its diff:
```python
import functools

import jax
import jax.numpy as jnp
from jax import lax
from jax.experimental import pallas as pl
from jax.experimental.pallas import tpu as pltpu
from jax.sharding import PartitionSpec as P


FIELDS = 4
LEVELS = 2
STEPS = 4
CH = FIELDS * LEVELS
ROWS = 32
GRID = 1024
BANDS = 32
QUARTERS = BANDS // CH
COLS = GRID // QUARTERS
PLANES = 4
F32 = jnp.float32
BF16 = jnp.bfloat16


def in_hbm(*arrays):
    return [pltpu.with_memory_space_constraint(a, pltpu.HBM) for a in arrays]


def start_all(pairs, sem):
    copies = [pltpu.make_async_copy(src, dst, sem.at[i]) for i, (src, dst) in enumerate(pairs)]
    for copy in copies:
        copy.start()
    return copies


def params(mib):
    return pltpu.CompilerParams(vmem_limit_bytes=mib << 20)


VMEM = pl.BlockSpec(memory_space=pltpu.VMEM)
SMEM = pl.BlockSpec(memory_space=pltpu.SMEM)
HBM = pl.BlockSpec(memory_space=pltpu.HBM)
EDGE = jax.ShapeDtypeStruct((CH // 2 + 1, 8, GRID), F32)


def pack_kernel(x_hbm, v_hbm, lo_ref, hi_ref, xe, ve, sem):
    pairs = [
        (src.at[:, at : at + 8], dst.at[j]) for src, dst in ((x_hbm, xe), (v_hbm, ve)) for j, at in enumerate((0, ROWS - 8))
    ]
    for copy in start_all(pairs, sem):
        copy.wait()
    row = lax.broadcasted_iota(jnp.int32, (8, GRID), 0)
    for k in range(CH // 2 + 1):
        ref, at = (xe, 2 * k) if k < CH // 2 else (ve, 0)
        lo_ref[k] = jnp.where(row < 4, ref[0, at], pltpu.roll(ref[0, at + 1], 4, 0))
        hi_ref[k] = jnp.where(row < 4, pltpu.roll(ref[1, at], 4, 0), ref[1, at + 1])


def pack_edges(x, v):
    return pl.pallas_call(
        pack_kernel,
        out_shape=(EDGE, EDGE),
        in_specs=[HBM, HBM],
        out_specs=(VMEM, VMEM),
        scratch_shapes=[
            pltpu.VMEM((2, CH, 8, GRID), F32),
            pltpu.VMEM((2, 2, 8, GRID), F32),
            pltpu.SemaphoreType.DMA((4,)),
        ],
        compiler_params=params(3),
        name="pack_edges",
    )(*in_hbm(x, v))


def stencil_kernel(base, k_ref, band_ref, x_hbm, v_hbm, before_hbm, after_hbm, o_ref, first, second, buf, vel, x_ref, v_ref, *edges):
    before_ref, after_ref, sem = edges
    pairs = ((before_hbm, before_ref), (after_hbm, after_ref), (v_hbm, v_ref), (x_hbm.at[base : base + CH // 2], x_ref))
    for copy in start_all(pairs, sem):
        copy.wait()
    row = lax.broadcasted_iota(jnp.int32, (8, GRID), 0)

    def edge(above, below, odd):
        swap = lambda t: pltpu.roll(t, 4, 0)
        pick = lambda a, b: jnp.where(row < 4, b, a)
        return pick(above, swap(below)) if odd else pick(swap(above), below)

    for d in range(2):
        vel[d, 0:8] = 0.5 * edge(before_ref[CH // 2], after_ref[CH // 2], d)
        vel[d, 8:40] = 0.5 * v_ref[d]
    band = band_ref[0]
    within = jnp.where(row < 4, (band < BANDS - 1).astype(F32), (band > 0).astype(F32))

    def field(pair, odd):
        c = 2 * pair + odd
        pairs_ref = (first, second)[pair]
        k = k_ref[base + c]
        outer = k * within
        fringe = edge(before_ref[base // 2 + pair], after_ref[base // 2 + pair], odd)
        buf[0, 0:8] = fringe
        buf[0, 8:40] = x_ref[c]
        buf[0, 40:48] = fringe
        for s in range(STEPS):
            src, dst = s % 2, (s + 1) % 2
            last = s == STEPS - 1
            for t in range(1 if last else 0, 5):
                r = 8 * t
                kk = k if t else outer
                x = buf[src, r : r + 8]
                up = buf[src, r + 1 : r + 9]
                lo = buf[src, r - 1 : r + 7] if t else buf[src, 39:47]
                e = pltpu.roll(x, GRID - 1, 1)
                w = pltpu.roll(x, 1, 1)
                y = x - vel[0, r : r + 8] * (e - w) - vel[1, r : r + 8] * (up - lo)
                y = y + kk * (up + lo + e + w - 4.0 * x)
                if last:
                    o_ref[c, r - 8 : r] = y
                    pairs_ref[odd, r - 8 : r] = y
                else:
                    buf[dst, r : r + 8] = y
                    if t == 0:
                        buf[dst, 40:48] = y

    for pair in range(2):
        field(pair, 0)
        field(pair, 1)


def propagate(base, x, v, before, after, diffuse, band):
    return pl.pallas_call(
        functools.partial(stencil_kernel, base),
        out_shape=tuple(jax.ShapeDtypeStruct((n, ROWS, GRID), F32) for n in (4, 2, 2)),
        in_specs=[SMEM, SMEM, HBM, HBM, HBM, HBM],
        out_specs=(VMEM, VMEM, VMEM),
        scratch_shapes=[
            pltpu.VMEM((2, 48, GRID), F32),
            pltpu.VMEM((2, 40, GRID), F32),
            pltpu.VMEM((CH // 2, ROWS, GRID), F32),
            pltpu.VMEM((2, ROWS, GRID), F32),
            pltpu.VMEM(EDGE.shape, F32),
            pltpu.VMEM(EDGE.shape, F32),
            pltpu.SemaphoreType.DMA((4,)),
        ],
        compiler_params=params(4),
        name="propagate",
    )(diffuse, band, *in_hbm(x, v, before, after))


def combine_kernel(x_ref, along0, along1, p0, p1, p2, p3, s_ref, o_hbm, buf, sem):
    half = CH // 2
    copies = []
    for c in range(CH):
        arrived = (along0 if c < half else along1)[c % half] + (p0, p1, p2, p3)[c // 2][c % 2]
        y = s_ref[c] * (x_ref[c] - arrived)
        at = slice(c * QUARTERS, (c + 1) * QUARTERS)
        for q in range(QUARTERS):
            buf[c * QUARTERS + q] = y[:, q * COLS : (q + 1) * COLS]
        copy = pltpu.make_async_copy(buf.at[at], o_hbm.at[at], sem.at[c])
        copy.start()
        copies.append(copy)
    for copy in copies:
        copy.wait()


def combine(x, arrived, sigma):
    return pl.pallas_call(
        combine_kernel,
        out_shape=jax.ShapeDtypeStruct((BANDS, ROWS, COLS), F32),
        in_specs=[VMEM] * 8,
        out_specs=HBM,
        scratch_shapes=[pltpu.VMEM((BANDS, ROWS, COLS), F32), pltpu.SemaphoreType.DMA((CH,))],
        compiler_params=params(3),
        name="combine",
    )(x, *arrived, sigma)


def halves(x):
    hi = x.astype(BF16)
    return hi, (x - hi.astype(F32)).astype(BF16)


def deal_kernel(c_hbm, o_ref, c_ref, sem):
    for copy in start_all(((c_hbm, c_ref),), sem):
        copy.wait()
    for d in range(BANDS):
        at = quarter_of(d) * COLS
        o_ref[d] = c_ref[:, at : at + COLS]


def quarter_of(band):
    return (band & 1) * 2 + band // (BANDS // 2)


def deal(c):
    return pl.pallas_call(
        deal_kernel,
        out_shape=jax.ShapeDtypeStruct((BANDS, ROWS, COLS), F32),
        in_specs=[HBM],
        out_specs=VMEM,
        scratch_shapes=[pltpu.VMEM((ROWS, GRID), F32), pltpu.SemaphoreType.DMA((1,))],
        compiler_params=params(2),
        name="deal",
    )(*in_hbm(c))


def rows_kernel(quarter_ref, own, beside, across, both, x_ref, o_ref, hi_ref, lo_ref, xh, xl):
    @pl.when(pl.program_id(0) == 0)
    def _():
        xh[...], xl[...] = halves(x_ref[...].reshape(GRID, COLS))

    for flip, ref in ((0, own), (1, beside), (2, across), (3, both)):
        at = pl.ds(pl.multiple_of((quarter_ref[0] ^ flip) * COLS, COLS), COLS)
        hi_ref[:, at], lo_ref[:, at] = halves(ref[...].reshape(256, COLS))
    dot = lambda a, b: jnp.dot(a, b, preferred_element_type=F32)
    y = dot(hi_ref[...], xl[...]) + dot(lo_ref[...], xh[...]) + dot(hi_ref[...], xh[...])
    o_ref[...] = y.reshape(8, ROWS, COLS)


def mix_rows(quarter, blocks, x):
    block = pl.BlockSpec((8, ROWS, COLS), lambda i: (i, 0, 0))
    whole = pl.BlockSpec((256, GRID), lambda i: (i, 0))
    shape = jax.ShapeDtypeStruct((GRID, GRID), BF16)
    return pl.pallas_call(
        rows_kernel,
        grid=(GRID // 256,),
        out_shape=(jax.ShapeDtypeStruct((BANDS, ROWS, COLS), F32), shape, shape),
        in_specs=[SMEM] + [block] * QUARTERS + [pl.BlockSpec((BANDS, ROWS, COLS), lambda i: (0, 0, 0))],
        out_specs=(block, whole, whole),
        scratch_shapes=[pltpu.VMEM((GRID, COLS), BF16)] * 2,
        compiler_params=params(12),
        name="mix_rows",
    )(quarter, *blocks, x)


def columns_kernel(hi_ref, lo_ref, r_ref, s_ref, o_ref, rh, rl):
    for c in range(CH):
        for q in range(QUARTERS):
            at = slice(c * ROWS, (c + 1) * ROWS), slice(q * COLS, (q + 1) * COLS)
            rh[at], rl[at] = halves(r_ref[c * QUARTERS + q])

    dot = lambda a, b: lax.dot_general(a, b, (((1,), (1,)), ((), ())), preferred_element_type=F32)

    @pl.loop(0, GRID // 256)
    def _(i):
        at = pl.ds(pl.multiple_of(i * 256, 256), 256)
        hi, lo = hi_ref[at], lo_ref[at]
        y = dot(rl[...], hi) + dot(rh[...], lo) + dot(rh[...], hi)
        o_ref[:, :, at] = s_ref[:, :, at] * y.reshape(CH, ROWS, 256)


def mix_columns(hi, lo, r, sigma):
    return pl.pallas_call(
        columns_kernel,
        out_shape=jax.ShapeDtypeStruct((CH, ROWS, GRID), F32),
        in_specs=[VMEM] * 4,
        out_specs=VMEM,
        scratch_shapes=[pltpu.VMEM((CH * ROWS, GRID), BF16)] * 2,
        compiler_params=params(4),
        name="mix_columns",
    )(hi, lo, r, sigma)


def to_next_window(ends):
    windows = lax.axis_size("tm")
    last = range(PLANES - 1, windows - 1, PLANES)
    along = [(i, i + 1) for i in range(windows - 1) if (i + 1) % PLANES]
    quarters = [pair for _, *pairs in ends for pair in pairs]
    arrived, relayed = [], []
    for half, *_ in ends:
        arrived.append(lax.ppermute(half, "tm", along))
    for plane, quarter in zip((0, 2, 1, PLANES - 1), quarters):
        if plane != PLANES - 1:
            quarter = lax.ppermute(quarter, "tm", [(w, w + 1 - PLANES + plane) for w in last])
        relayed.append(lax.ppermute(quarter, "tm", [(w + 1 - PLANES + plane, w + 1) for w in last]))
    return arrived + relayed


def gather_correlation(correlation):
    own = lax.all_to_all(deal(correlation), "band", 0, 0, tiled=True)
    far, near = BANDS // 2, 1
    beside = lax.ppermute(own, "band", [(b, b ^ far) for b in range(BANDS)])
    across = lax.ppermute(own, "band", [(b, b ^ near) for b in range(BANDS)])
    return own, beside, across, lax.ppermute(beside, "band", [(b, b ^ near) for b in range(BANDS)])


def defects(increments, velocity, diffusivity, scaling, correlation):
    x = increments.reshape(CH, ROWS, GRID)
    v = velocity[0]
    sigma = scaling.reshape(CH, ROWS, GRID)
    up = [(i, i + 1) for i in range(BANDS - 1)]
    down = [(j, i) for i, j in up]
    lo_edge, hi_edge = pack_edges(x, v)
    before = lax.ppermute(hi_edge, "band", up)
    after = lax.ppermute(lo_edge, "band", down)
    band = lax.axis_index("band").reshape(1)
    diffuse = diffusivity.reshape(CH)
    ends = []
    for base in (0, CH // 2):
        ends.append(propagate(base, x, v, before, after, diffuse, band))
    sent = combine(x, to_next_window(ends), sigma)
    blocks = gather_correlation(correlation)
    mine = lax.all_to_all(sent, "band", 0, 0, tiled=True)
    mixed, hi, lo = mix_rows(quarter_of(band), blocks, mine)
    back = lax.all_to_all(mixed, "band", 0, 0, tiled=True)
    return mix_columns(hi, lo, back, sigma).reshape(1, FIELDS, LEVELS, ROWS, GRID)


def solution(mesh):
    return jax.shard_map(
        defects,
        mesh=mesh,
        in_specs=(
            P("tm", None, None, "band", None),
            P("tm", None, "band", None),
            P(),
            P(None, None, "band", None),
            P("band", None),
        ),
        out_specs=P("tm", None, None, "band", None),
        check_vma=False,
    )
```

time: 239 us -> 174 us (0.73)
  the two profiles are of different devices: /device:TPU:264 before, /device:TPU:136 now
where the time goes in v2:
time: 174 us
  starting transfers between devices  58.2 us (33%)
  waiting for transfers between devices  55.4 us (32%)
  blocking collectives  32.2 us (19%)
  Pallas kernels  25.6 us (15%)
  local copies, waits for them, and re-layouts  1.84 us (1%)
    all_to_all x1, blocking collectives, defects(): back = lax.all_to_all(mixed, 'band', 0, 0, tiled=True)  32.2 us
    all_to_all x1, waiting for transfers between devices, defects(): mine = lax.all_to_all(sent, 'band', 0, 0, tiled=True)  21.3 us
    ppermute x1, waiting for transfers between devices, defects(): before = lax.ppermute(hi_edge, 'band', up)  18 us
    all_to_all x1, starting transfers between devices, defects(): mine = lax.all_to_all(sent, 'band', 0, 0, tiled=True)  12.8 us
    ppermute x4, starting transfers between devices, to_next_window(): lax.ppermute(quarter, 'tm', [(w + 1 - PLANES + plane, w + 1) for w in last])  10.9 us
    pallas_call x2, Pallas kernels, propagate(): pl.pallas_call(functools.partial(stencil_kernel, base), out_shape=tuple((...  10.9 us
    all_to_all x1, starting transfers between devices, gather_correlation(): own = lax.all_to_all(deal(correlation), 'band', 0, 0, tiled=True)  9.53 us
    ppermute x2, starting transfers between devices, to_next_window(): arrived.append(lax.ppermute(half, 'tm', along))  7.03 us
  transfers between devices with their start and end apart: 16, of which 6 were waited for; matrix products, arithmetic and copies ran while one was open for 0% of the time, Pallas kernels for 9%

profile of v2, /device:TPU:136, one launch (start us, length us, event | category | flops | bytes accessed | tf_op | source)
XLA Modules:
  0.0 173.5 jit_solution(3671720926146029857)
XLA Ops:
  0.0 2.0 %deal.1 = f32[32,32,256]{2,1,0:T(8,128)} custom-call(f32[32,1024]{1,0:T(8,128)} %c_hbm.1), custom_call_target="tpu_custom_call" | custom-call | tf_op jit(solution)/shard_map/deal/pallas_call | solution.py:194
  2.0 9.5 %all-to-all-start = ((f32[32,32,256]{2,1,0:T(8,128)}), f32[32,32,256]{2,1,0:T(8,128)S(1)}, u32[]{:S(2)}, u32[]{:S(2)}) async-start(f32[32,32,256]{2,1,0:T(8,128)} %deal.1), calls=%async_computation | async-start | bytes 2097152 | tf_op jit(solution)/shard_map/all_to_all | solution.py:278
  11.5 0.0 copy-start
  11.5 0.0 copy-start.1
  11.5 1.9 %pack_edges.1 = (f32[5,8,1024]{2,1,0:T(8,128)S(1)}, f32[5,8,1024]{2,1,0:T(8,128)}) custom-call(f32[8,32,1024]{2,1,0:T(8,128)} %bitcast.5, f32[2,32,1024]{2,1,0:T(8,128)} %bitcast.11), custom_call_target="tpu_custom_call" | custom-call | tf_op jit(solution)/shard_map/pack_edges/pallas_call | solution.py:60
  13.4 2.0 %collective-permute-start.3 = (f32[5,8,1024]{2,1,0:T(8,128)}, f32[5,8,1024]{2,1,0:T(8,128)}, u32[]{:S(2)}, u32[]{:S(2)}) collective-permute-start(f32[5,8,1024]{2,1,0:T(8,128)} %get-tuple-element.16), channel_id=1, source_target_pairs={{0,1},{1,2},{2,3},{3,4},{4,5},{5,6},{6,7},{7,8},{8,9},{9,10},{10,1... | collective-permute-start | bytes 491528 | tf_op jit(solution)/shard_map/ppermute | solution.py:292
  15.5 3.5 %collective-permute-start.4 = (f32[5,8,1024]{2,1,0:T(8,128)S(1)}, f32[5,8,1024]{2,1,0:T(8,128)}, u32[]{:S(2)}, u32[]{:S(2)}) collective-permute-start(f32[5,8,1024]{2,1,0:T(8,128)S(1)} %get-tuple-element.17), channel_id=1, source_target_pairs={{1,0},{2,1},{3,2},{4,3},{5,4},{6,5},{7,6},{8,7},{9,8},{10,9},{11,1... | collective-permute-start | bytes 491528 | tf_op jit(solution)/shard_map/ppermute | solution.py:293
  19.0 0.0 copy-done.4
  19.0 0.1 copy.7
  19.1 0.1 reshape.21.k_ref
  19.2 18.0 %collective-permute-done.3.before_hbm = f32[5,8,1024]{2,1,0:T(8,128)} collective-permute-done((f32[5,8,1024]{2,1,0:T(8,128)}, f32[5,8,1024]{2,1,0:T(8,128)}, u32[]{:S(2)}, u32[]{:S(2)}) %collective-permute-start.3) | collective-permute-done | bytes 163872 | tf_op jit(solution)/shard_map/ppermute | solution.py:292
  37.2 0.0 collective-permute-done.4.after_hbm
  37.2 5.4 %propagate.3 = (f32[4,32,1024]{2,1,0:T(8,128)}, f32[2,32,1024]{2,1,0:T(8,128)S(1)}, f32[2,32,1024]{2,1,0:T(8,128)S(1)}) custom-call(f32[8]{0:T(128)S(1)} %reshape.21.k_ref, s32[1]{0:T(128)} %bitcast.band_ref, f32[8,32,1024]{2,1,0:T(8,128)} %bitcast.6, f32[2,32,1024]{2,1,0:T(8,128)} %bitcast.12, f32[5,8,1024]{2,1,0:T(8,128)} %collective-permute-done.3.before_hbm, ...), custom_call_target="tpu_custom_call" | custom-call | tf_op jit(solution)/shard_map/propagate/pallas_call | solution.py:129
  42.7 0.7 collective-permute-start.11
  43.4 1.3 collective-permute-start.13
  44.7 4.2 %collective-permute-start.6 = (f32[4,32,1024]{2,1,0:T(8,128)}, f32[4,32,1024]{2,1,0:T(8,128)}, u32[]{:S(2)}, u32[]{:S(2)}) collective-permute-start(f32[4,32,1024]{2,1,0:T(8,128)} %get-tuple-element.19), channel_id=1, source_target_pairs={{0,32},{32,64},{64,96},{128,160},{160,192},{192,224},{256,288},{28... | collective-permute-start | bytes 1572872 | tf_op jit(solution)/shard_map/ppermute | solution.py:269
  48.9 5.4 %propagate.2 = (f32[4,32,1024]{2,1,0:T(8,128)}, f32[2,32,1024]{2,1,0:T(8,128)S(1)}, f32[2,32,1024]{2,1,0:T(8,128)S(1)}) custom-call(f32[8]{0:T(128)S(1)} %reshape.21.k_ref, s32[1]{0:T(128)} %bitcast.band_ref, f32[8,32,1024]{2,1,0:T(8,128)} %bitcast.7, f32[2,32,1024]{2,1,0:T(8,128)} %bitcast.13, f32[5,8,1024]{2,1,0:T(8,128)} %collective-permute-done.3.before_hbm, ...), custom_call_target="tpu_custom_call" | custom-call | tf_op jit(solution)/shard_map/propagate/pallas_call | solution.py:129
  54.3 1.3 collective-permute-start.7
  55.6 1.4 collective-permute-start.9
  57.0 0.0 collective-permute-done.11
  57.0 2.8 %collective-permute-start.5 = (f32[4,32,1024]{2,1,0:T(8,128)}, f32[4,32,1024]{2,1,0:T(8,128)}, u32[]{:S(2)}, u32[]{:S(2)}) collective-permute-start(f32[4,32,1024]{2,1,0:T(8,128)} %get-tuple-element.18), channel_id=1, source_target_pairs={{0,32},{32,64},{64,96},{128,160},{160,192},{192,224},{256,288},{28... | collective-permute-start | bytes 1572872 | tf_op jit(solution)/shard_map/ppermute | solution.py:269
  59.8 0.0 collective-permute-done.13.p3
  59.8 1.3 collective-permute-start.12
  61.1 6.0 %collective-permute-done.7 = f32[2,32,1024]{2,1,0:T(8,128)} collective-permute-done((f32[2,32,1024]{2,1,0:T(8,128)S(1)}, f32[2,32,1024]{2,1,0:T(8,128)}, u32[]{:S(2)}, u32[]{:S(2)}) %collective-permute-start.7) | collective-permute-done | bytes 262176 | tf_op jit(solution)/shard_map/ppermute | solution.py:272
  67.1 7.1 %collective-permute-start.8 = (f32[2,32,1024]{2,1,0:T(8,128)}, f32[2,32,1024]{2,1,0:T(8,128)}, u32[]{:S(2)}, u32[]{:S(2)}) collective-permute-start(f32[2,32,1024]{2,1,0:T(8,128)} %collective-permute-done.7), channel_id=1, source_target_pairs={{0,128},{128,256},{256,384},{1,129},{129,257},{257,385},{2,130},{1... | collective-permute-start | bytes 786440 | tf_op jit(solution)/shard_map/ppermute | solution.py:273
  74.1 0.0 collective-permute-done.9
  74.2 1.3 collective-permute-start.10
  75.5 0.0 collective-permute-done.12.p2
  75.5 0.0 copy-start.2
  75.5 0.7 copy-done.2
  76.2 0.0 all-to-all-done.own
  76.2 5.1 %collective-permute-start = (f32[32,32,256]{2,1,0:T(8,128)S(1)}, f32[32,32,256]{2,1,0:T(8,128)}, u32[]{:S(2)}, u32[]{:S(2)}) collective-permute-start(f32[32,32,256]{2,1,0:T(8,128)S(1)} %all-to-all-done.own), channel_id=1, source_target_pairs={{0,16},{1,17},{2,18},{3,19},{4,20},{5,21},{6,22},{7,23},{8,24},{9,... | collective-permute-start | bytes 3145736 | tf_op jit(solution)/shard_map/ppermute | solution.py:280
  81.3 0.0 collective-permute-done.6.along1
  81.3 5.4 %collective-permute-done.8.p0 = f32[2,32,1024]{2,1,0:T(8,128)} collective-permute-done((f32[2,32,1024]{2,1,0:T(8,128)}, f32[2,32,1024]{2,1,0:T(8,128)}, u32[]{:S(2)}, u32[]{:S(2)}) %collective-permute-start.8) | collective-permute-done | bytes 262176 | tf_op jit(solution)/shard_map/ppermute | solution.py:273
  86.7 0.9 collective-permute-done.10.p1
  87.6 0.0 collective-permute-done.5.along0
  87.6 0.9 copy-done.3
  88.6 2.4 %combine.1 = f32[32,32,256]{2,1,0:T(8,128)} custom-call(f32[8,32,1024]{2,1,0:T(8,128)S(1)} %bitcast.8, f32[4,32,1024]{2,1,0:T(8,128)} %collective-permute-done.5.along0, f32[4,32,1024]{2,1,0:T(8,128)} %collective-permute-done.6.along1, f32[2,32,1024]{2,1,0:T(8,128)} %collective-permute-done.8.p0, f32[2,32,1024]{2,1,0:T(8,128)} %collective-permute-done.10.p1, ...), custom_call_target="tpu_custom_call" | custom-call | tf_op jit(solution)/shard_map/combine/pallas_call | solution.py:165
  91.0 12.8 %all-to-all-start.1 = ((f32[32,32,256]{2,1,0:T(8,128)}), f32[32,32,256]{2,1,0:T(8,128)S(1)}, u32[]{:S(2)}, u32[]{:S(2)}) async-start(f32[32,32,256]{2,1,0:T(8,128)} %combine.1), calls=%async_computation.1 | async-start | bytes 2097152 | tf_op jit(solution)/shard_map/all_to_all | solution.py:301
  103.8 2.0 %collective-permute-start.1 = (f32[32,32,256]{2,1,0:T(8,128)S(1)}, f32[32,32,256]{2,1,0:T(8,128)}, u32[]{:S(2)}, u32[]{:S(2)}) collective-permute-start(f32[32,32,256]{2,1,0:T(8,128)S(1)} %all-to-all-done.own), channel_id=1, source_target_pairs={{0,1},{1,0},{2,3},{3,2},{4,5},{5,4},{6,7},{7,6},{8,9},{9,8},{10,11... | collective-permute-start | bytes 3145736 | tf_op jit(solution)/shard_map/ppermute | solution.py:281
  105.8 3.7 %collective-permute-done.beside = f32[32,32,256]{2,1,0:T(8,128)} collective-permute-done((f32[32,32,256]{2,1,0:T(8,128)S(1)}, f32[32,32,256]{2,1,0:T(8,128)}, u32[]{:S(2)}, u32[]{:S(2)}) %collective-permute-start) | collective-permute-done | bytes 1048608 | tf_op jit(solution)/shard_map/ppermute | solution.py:280
  109.6 1.9 %collective-permute-start.2 = (f32[32,32,256]{2,1,0:T(8,128)}, f32[32,32,256]{2,1,0:T(8,128)}, u32[]{:S(2)}, u32[]{:S(2)}) collective-permute-start(f32[32,32,256]{2,1,0:T(8,128)} %collective-permute-done.beside), channel_id=1, source_target_pairs={{0,1},{1,0},{2,3},{3,2},{4,5},{5,4},{6,7},{7,6},{8,9},{9,8},{10,11... | collective-permute-start | bytes 3145736 | tf_op jit(solution)/shard_map/ppermute | solution.py:282
  111.5 21.3 %all-to-all-done.1.x_ref = f32[32,32,256]{2,1,0:T(8,128)S(1)} async-done(((f32[32,32,256]{2,1,0:T(8,128)}), f32[32,32,256]{2,1,0:T(8,128)S(1)}, u32[]{:S(2)}, u32[]{:S(2)}) %all-to-all-start.1) | async-done | bytes 1048608 | tf_op jit(solution)/shard_map/all_to_all | solution.py:301
  132.8 0.0 collective-permute-done.1.across
  132.8 0.0 collective-permute-done.2.both
  132.8 4.9 %mix_rows.1 = (f32[32,32,256]{2,1,0:T(8,128)S(1)}, bf16[1024,1024]{1,0:T(8,128)(2,1)S(1)}, bf16[1024,1024]{1,0:T(8,128)(2,1)S(1)}) custom-call(s32[1]{0:T(128)S(6)} %add.4.quarter_ref, f32[32,32,256]{2,1,0:T(8,128)S(1)} %all-to-all-done.own, f32[32,32,256]{2,1,0:T(8,128)} %collective-permute-done.beside, f32[32,32,256]{2,1,0:T(8,128)} %collective-permute-done.1.across, ...), custom_call_target="tpu_custom_call" | custom-call | tf_op jit(solution)/shard_map/mix_rows/pallas_call | solution.py:222
  137.7 32.2 %all_to_all.15.r_ref = f32[32,32,256]{2,1,0:T(8,128)S(1)} all-to-all(f32[32,32,256]{2,1,0:T(8,128)S(1)} %get-tuple-element.26), channel_id=1, replica_groups=mesh['tm'=16,'band'=32] {'band'}, dimensions={0} | all-to-all | bytes 2097152 | tf_op jit(solution)/shard_map/all_to_all | solution.py:303
  169.9 3.6 %mix_columns.1 = f32[8,32,1024]{2,1,0:T(8,128)} custom-call(bf16[1024,1024]{1,0:T(8,128)(2,1)S(1)} %get-tuple-element.24.hi_ref, bf16[1024,1024]{1,0:T(8,128)(2,1)S(1)} %get-tuple-element.25.lo_ref, f32[32,32,256]{2,1,0:T(8,128)S(1)} %all_to_all.15.r_ref, f32[8,32,1024]{2,1,0:T(8,128)S(1)} %bitcast.10), custom_call_target="tpu_custom_call" | custom-call | tf_op jit(solution)/shard_map/mix_columns/pallas_call | solution.py:251
  (4 shorter events, 0.0 us)
Async XLA Ops:
  0.0 19.0 %copy-start.4 = (f32[4,2]{0,1:T(2,128)S(1)}, f32[4,2]{0,1:T(2,128)}, u32[]{:S(2)}) copy-start(f32[4,2]{0,1:T(2,128)} %param.7) | copy-start | bytes 100
  2.0 74.2 %all-to-all-start = ((f32[32,32,256]{2,1,0:T(8,128)}), f32[32,32,256]{2,1,0:T(8,128)S(1)}, u32[]{:S(2)}, u32[]{:S(2)}) async-start(f32[32,32,256]{2,1,0:T(8,128)} %deal.1), calls=%async_computation | async-start | bytes 2097152 | tf_op jit(solution)/shard_map/all_to_all | solution.py:278
  11.5 76.1 %copy-start = (f32[1,4,2,32,1024]{4,3,2,1,0:T(8,128)S(1)}, f32[1,4,2,32,1024]{4,3,2,1,0:T(8,128)}, u32[]{:S(2)}) copy-start(f32[1,4,2,32,1024]{4,3,2,1,0:T(8,128)} %param.5) | copy-start | bytes 3145732
  11.5 76.1 %copy-start.1 = (f32[4,2,32,1024]{3,2,1,0:T(8,128)S(1)}, f32[4,2,32,1024]{3,2,1,0:T(8,128)}, u32[]{:S(2)}) copy-start(f32[4,2,32,1024]{3,2,1,0:T(8,128)} %param.8) | copy-start | bytes 3145732
  13.4 23.8 %collective-permute-start.3 = (f32[5,8,1024]{2,1,0:T(8,128)}, f32[5,8,1024]{2,1,0:T(8,128)}, u32[]{:S(2)}, u32[]{:S(2)}) collective-permute-start(f32[5,8,1024]{2,1,0:T(8,128)} %get-tuple-element.16), channel_id=1, source_target_pairs={{0,1},{1,2},{2,3},{3,4},{4,5},{5,6},{6,7},{7,8},{8,9},{9,10},{10,1... | collective-permute-start | bytes 491528 | tf_op jit(solution)/shard_map/ppermute | solution.py:292
  15.5 21.8 %collective-permute-start.4 = (f32[5,8,1024]{2,1,0:T(8,128)S(1)}, f32[5,8,1024]{2,1,0:T(8,128)}, u32[]{:S(2)}, u32[]{:S(2)}) collective-permute-start(f32[5,8,1024]{2,1,0:T(8,128)S(1)} %get-tuple-element.17), channel_id=1, source_target_pairs={{1,0},{2,1},{3,2},{4,3},{5,4},{6,5},{7,6},{8,7},{9,8},{10,9},{11,1... | collective-permute-start | bytes 491528 | tf_op jit(solution)/shard_map/ppermute | solution.py:293
  42.7 14.3 %collective-permute-start.11 = (f32[2,32,1024]{2,1,0:T(8,128)S(1)}, f32[2,32,1024]{2,1,0:T(8,128)S(1)}, u32[]{:S(2)}, u32[]{:S(2)}) collective-permute-start(f32[2,32,1024]{2,1,0:T(8,128)S(1)} %get-tuple-element.22), channel_id=1, source_target_pairs={{96,32},{224,160},{352,288},{97,33},{225,161},{353,289},{98,34},{2... | collective-permute-start | bytes 786440 | tf_op jit(solution)/shard_map/ppermute | solution.py:272
  43.4 16.4 %collective-permute-start.13 = (f32[2,32,1024]{2,1,0:T(8,128)S(1)}, f32[2,32,1024]{2,1,0:T(8,128)S(1)}, u32[]{:S(2)}, u32[]{:S(2)}) collective-permute-start(f32[2,32,1024]{2,1,0:T(8,128)S(1)} %get-tuple-element.23), channel_id=1, source_target_pairs={{96,128},{224,256},{352,384},{97,129},{225,257},{353,385},{98,130}... | collective-permute-start | bytes 786440 | tf_op jit(solution)/shard_map/ppermute | solution.py:273
  44.7 36.6 %collective-permute-start.6 = (f32[4,32,1024]{2,1,0:T(8,128)}, f32[4,32,1024]{2,1,0:T(8,128)}, u32[]{:S(2)}, u32[]{:S(2)}) collective-permute-start(f32[4,32,1024]{2,1,0:T(8,128)} %get-tuple-element.19), channel_id=1, source_target_pairs={{0,32},{32,64},{64,96},{128,160},{160,192},{192,224},{256,288},{28... | collective-permute-start | bytes 1572872 | tf_op jit(solution)/shard_map/ppermute | solution.py:269
  54.3 12.8 %collective-permute-start.7 = (f32[2,32,1024]{2,1,0:T(8,128)S(1)}, f32[2,32,1024]{2,1,0:T(8,128)}, u32[]{:S(2)}, u32[]{:S(2)}) collective-permute-start(f32[2,32,1024]{2,1,0:T(8,128)S(1)} %get-tuple-element.20), channel_id=1, source_target_pairs={{96,0},{224,128},{352,256},{97,1},{225,129},{353,257},{98,2},{226,... | collective-permute-start | bytes 786440 | tf_op jit(solution)/shard_map/ppermute | solution.py:272
  55.6 18.5 %collective-permute-start.9 = (f32[2,32,1024]{2,1,0:T(8,128)S(1)}, f32[2,32,1024]{2,1,0:T(8,128)}, u32[]{:S(2)}, u32[]{:S(2)}) collective-permute-start(f32[2,32,1024]{2,1,0:T(8,128)S(1)} %get-tuple-element.21), channel_id=1, source_target_pairs={{96,64},{224,192},{352,320},{97,65},{225,193},{353,321},{98,66},{2... | collective-permute-start | bytes 786440 | tf_op jit(solution)/shard_map/ppermute | solution.py:272
  57.0 30.6 %collective-permute-start.5 = (f32[4,32,1024]{2,1,0:T(8,128)}, f32[4,32,1024]{2,1,0:T(8,128)}, u32[]{:S(2)}, u32[]{:S(2)}) collective-permute-start(f32[4,32,1024]{2,1,0:T(8,128)} %get-tuple-element.18), channel_id=1, source_target_pairs={{0,32},{32,64},{64,96},{128,160},{160,192},{192,224},{256,288},{28... | collective-permute-start | bytes 1572872 | tf_op jit(solution)/shard_map/ppermute | solution.py:269
  59.8 15.7 %collective-permute-start.12 = (f32[2,32,1024]{2,1,0:T(8,128)S(1)}, f32[2,32,1024]{2,1,0:T(8,128)S(1)}, u32[]{:S(2)}, u32[]{:S(2)}) collective-permute-start(f32[2,32,1024]{2,1,0:T(8,128)S(1)} %collective-permute-done.11), channel_id=1, source_target_pairs={{32,128},{160,256},{288,384},{33,129},{161,257},{289,385},{34,130}... | collective-permute-start | bytes 786440 | tf_op jit(solution)/shard_map/ppermute | solution.py:273
  67.1 19.6 %collective-permute-start.8 = (f32[2,32,1024]{2,1,0:T(8,128)}, f32[2,32,1024]{2,1,0:T(8,128)}, u32[]{:S(2)}, u32[]{:S(2)}) collective-permute-start(f32[2,32,1024]{2,1,0:T(8,128)} %collective-permute-done.7), channel_id=1, source_target_pairs={{0,128},{128,256},{256,384},{1,129},{129,257},{257,385},{2,130},{1... | collective-permute-start | bytes 786440 | tf_op jit(solution)/shard_map/ppermute | solution.py:273
  74.2 13.5 %collective-permute-start.10 = (f32[2,32,1024]{2,1,0:T(8,128)}, f32[2,32,1024]{2,1,0:T(8,128)}, u32[]{:S(2)}, u32[]{:S(2)}) collective-permute-start(f32[2,32,1024]{2,1,0:T(8,128)} %collective-permute-done.9), channel_id=1, source_target_pairs={{64,128},{192,256},{320,384},{65,129},{193,257},{321,385},{66,130}... | collective-permute-start | bytes 786440 | tf_op jit(solution)/shard_map/ppermute | solution.py:273
  75.5 0.7 copy-start.2
  76.2 33.4 %collective-permute-start = (f32[32,32,256]{2,1,0:T(8,128)S(1)}, f32[32,32,256]{2,1,0:T(8,128)}, u32[]{:S(2)}, u32[]{:S(2)}) collective-permute-start(f32[32,32,256]{2,1,0:T(8,128)S(1)} %all-to-all-done.own), channel_id=1, source_target_pairs={{0,16},{1,17},{2,18},{3,19},{4,20},{5,21},{6,22},{7,23},{8,24},{9,... | collective-permute-start | bytes 3145736 | tf_op jit(solution)/shard_map/ppermute | solution.py:280
  87.6 1.0 copy-start.3
  91.0 41.8 %all-to-all-start.1 = ((f32[32,32,256]{2,1,0:T(8,128)}), f32[32,32,256]{2,1,0:T(8,128)S(1)}, u32[]{:S(2)}, u32[]{:S(2)}) async-start(f32[32,32,256]{2,1,0:T(8,128)} %combine.1), calls=%async_computation.1 | async-start | bytes 2097152 | tf_op jit(solution)/shard_map/all_to_all | solution.py:301
  103.8 29.0 %collective-permute-start.1 = (f32[32,32,256]{2,1,0:T(8,128)S(1)}, f32[32,32,256]{2,1,0:T(8,128)}, u32[]{:S(2)}, u32[]{:S(2)}) collective-permute-start(f32[32,32,256]{2,1,0:T(8,128)S(1)} %all-to-all-done.own), channel_id=1, source_target_pairs={{0,1},{1,0},{2,3},{3,2},{4,5},{5,4},{6,7},{7,6},{8,9},{9,8},{10,11... | collective-permute-start | bytes 3145736 | tf_op jit(solution)/shard_map/ppermute | solution.py:281
  109.6 23.2 %collective-permute-start.2 = (f32[32,32,256]{2,1,0:T(8,128)}, f32[32,32,256]{2,1,0:T(8,128)}, u32[]{:S(2)}, u32[]{:S(2)}) collective-permute-start(f32[32,32,256]{2,1,0:T(8,128)} %collective-permute-done.beside), channel_id=1, source_target_pairs={{0,1},{1,0},{2,3},{3,2},{4,5},{5,4},{6,7},{7,6},{8,9},{9,8},{10,11... | collective-permute-start | bytes 3145736 | tf_op jit(solution)/shard_map/ppermute | solution.py:282

commit v3 on v2

--- a/solution.py
+++ b/solution.py
@@ -72,11 +72,7 @@
     )(*in_hbm(x, v))
 
 
-def stencil_kernel(base, k_ref, band_ref, x_hbm, v_hbm, before_hbm, after_hbm, o_ref, first, second, buf, vel, x_ref, v_ref, *edges):
-    before_ref, after_ref, sem = edges
-    pairs = ((before_hbm, before_ref), (after_hbm, after_ref), (v_hbm, v_ref), (x_hbm.at[base : base + CH // 2], x_ref))
-    for copy in start_all(pairs, sem):
-        copy.wait()
+def stencil_kernel(base, k_ref, band_ref, x_ref, v_ref, before_ref, after_ref, o_ref, first, second, buf, vel):
     row = lax.broadcasted_iota(jnp.int32, (8, GRID), 0)
 
     def edge(above, below, odd):
@@ -97,7 +93,7 @@
         outer = k * within
         fringe = edge(before_ref[base // 2 + pair], after_ref[base // 2 + pair], odd)
         buf[0, 0:8] = fringe
-        buf[0, 8:40] = x_ref[c]
+        buf[0, 8:40] = x_ref[base + c]
         buf[0, 40:48] = fringe
         for s in range(STEPS):
             src, dst = s % 2, (s + 1) % 2
@@ -129,20 +125,12 @@
     return pl.pallas_call(
         functools.partial(stencil_kernel, base),
         out_shape=tuple(jax.ShapeDtypeStruct((n, ROWS, GRID), F32) for n in (4, 2, 2)),
-        in_specs=[SMEM, SMEM, HBM, HBM, HBM, HBM],
+        in_specs=[SMEM, SMEM, VMEM, VMEM, VMEM, VMEM],
         out_specs=(VMEM, VMEM, VMEM),
-        scratch_shapes=[
-            pltpu.VMEM((2, 48, GRID), F32),
-            pltpu.VMEM((2, 40, GRID), F32),
-            pltpu.VMEM((CH // 2, ROWS, GRID), F32),
-            pltpu.VMEM((2, ROWS, GRID), F32),
-            pltpu.VMEM(EDGE.shape, F32),
-            pltpu.VMEM(EDGE.shape, F32),
-            pltpu.SemaphoreType.DMA((4,)),
-        ],
-        compiler_params=params(4),
+        scratch_shapes=[pltpu.VMEM((2, 48, GRID), F32), pltpu.VMEM((2, 40, GRID), F32)],
+        compiler_params=params(2),
         name="propagate",
-    )(diffuse, band, *in_hbm(x, v, before, after))
+    )(diffuse, band, x, v, before, after)
 
 
 def combine_kernel(x_ref, along0, along1, p0, p1, p2, p3, s_ref, o_hbm, buf, sem):
@@ -178,60 +166,33 @@
     return hi, (x - hi.astype(F32)).astype(BF16)
 
 
-def deal_kernel(c_hbm, o_ref, c_ref, sem):
-    for copy in start_all(((c_hbm, c_ref),), sem):
-        copy.wait()
-    for d in range(BANDS):
-        at = quarter_of(d) * COLS
-        o_ref[d] = c_ref[:, at : at + COLS]
-
-
-def quarter_of(band):
-    return (band & 1) * 2 + band // (BANDS // 2)
-
-
-def deal(c):
-    return pl.pallas_call(
-        deal_kernel,
-        out_shape=jax.ShapeDtypeStruct((BANDS, ROWS, COLS), F32),
-        in_specs=[HBM],
-        out_specs=VMEM,
-        scratch_shapes=[pltpu.VMEM((ROWS, GRID), F32), pltpu.SemaphoreType.DMA((1,))],
-        compiler_params=params(2),
-        name="deal",
-    )(*in_hbm(c))
-
-
-def rows_kernel(quarter_ref, own, beside, across, both, x_ref, o_ref, hi_ref, lo_ref, xh, xl):
+def rows_kernel(c_ref, x_ref, o_ref, hi_ref, lo_ref, xh, xl):
     @pl.when(pl.program_id(0) == 0)
     def _():
         xh[...], xl[...] = halves(x_ref[...].reshape(GRID, COLS))
 
-    for flip, ref in ((0, own), (1, beside), (2, across), (3, both)):
-        at = pl.ds(pl.multiple_of((quarter_ref[0] ^ flip) * COLS, COLS), COLS)
-        hi_ref[:, at], lo_ref[:, at] = halves(ref[...].reshape(256, COLS))
+    hi_ref[...], lo_ref[...] = halves(c_ref[...])
     dot = lambda a, b: jnp.dot(a, b, preferred_element_type=F32)
     y = dot(hi_ref[...], xl[...]) + dot(lo_ref[...], xh[...]) + dot(hi_ref[...], xh[...])
     o_ref[...] = y.reshape(8, ROWS, COLS)
 
 
-def mix_rows(quarter, blocks, x):
-    block = pl.BlockSpec((8, ROWS, COLS), lambda i: (i, 0, 0))
+def mix_rows(c, x):
     whole = pl.BlockSpec((256, GRID), lambda i: (i, 0))
     shape = jax.ShapeDtypeStruct((GRID, GRID), BF16)
     return pl.pallas_call(
         rows_kernel,
         grid=(GRID // 256,),
         out_shape=(jax.ShapeDtypeStruct((BANDS, ROWS, COLS), F32), shape, shape),
-        in_specs=[SMEM] + [block] * QUARTERS + [pl.BlockSpec((BANDS, ROWS, COLS), lambda i: (0, 0, 0))],
-        out_specs=(block, whole, whole),
+        in_specs=[whole, pl.BlockSpec((BANDS, ROWS, COLS), lambda i: (0, 0, 0))],
+        out_specs=(pl.BlockSpec((8, ROWS, COLS), lambda i: (i, 0, 0)), whole, whole),
         scratch_shapes=[pltpu.VMEM((GRID, COLS), BF16)] * 2,
         compiler_params=params(12),
         name="mix_rows",
-    )(quarter, *blocks, x)
-
-
-def columns_kernel(hi_ref, lo_ref, r_ref, s_ref, o_ref, rh, rl):
+    )(*in_hbm(c), x)
+
+
+def columns_kernel(hi_ref, lo_ref, r_ref, s_ref, o_hbm, rh, rl, buf, sem):
     for c in range(CH):
         for q in range(QUARTERS):
             at = slice(c * ROWS, (c + 1) * ROWS), slice(q * COLS, (q + 1) * COLS)
@@ -239,12 +200,16 @@
 
     dot = lambda a, b: lax.dot_general(a, b, (((1,), (1,)), ((), ())), preferred_element_type=F32)
 
-    @pl.loop(0, GRID // 256)
-    def _(i):
-        at = pl.ds(pl.multiple_of(i * 256, 256), 256)
+    copies = []
+    for i in range(GRID // 256):
+        at = slice(i * 256, (i + 1) * 256)
         hi, lo = hi_ref[at], lo_ref[at]
         y = dot(rl[...], hi) + dot(rh[...], lo) + dot(rh[...], hi)
-        o_ref[:, :, at] = s_ref[:, :, at] * y.reshape(CH, ROWS, 256)
+        buf[:, :, at] = s_ref[:, :, at] * y.reshape(CH, ROWS, 256)
+        copies.append(pltpu.make_async_copy(buf.at[:, :, at], o_hbm.at[:, :, at], sem.at[i]))
+        copies[i].start()
+    for copy in copies:
+        copy.wait()
 
 
 def mix_columns(hi, lo, r, sigma):
@@ -252,9 +217,10 @@
         columns_kernel,
         out_shape=jax.ShapeDtypeStruct((CH, ROWS, GRID), F32),
         in_specs=[VMEM] * 4,
-        out_specs=VMEM,
-        scratch_shapes=[pltpu.VMEM((CH * ROWS, GRID), BF16)] * 2,
-        compiler_params=params(4),
+        out_specs=HBM,
+        scratch_shapes=[pltpu.VMEM((CH * ROWS, GRID), BF16)] * 2
+        + [pltpu.VMEM((CH, ROWS, GRID), F32), pltpu.SemaphoreType.DMA((GRID // 256,))],
+        compiler_params=params(5),
         name="mix_columns",
     )(hi, lo, r, sigma)
 
@@ -267,19 +233,11 @@
     arrived, relayed = [], []
     for half, *_ in ends:
         arrived.append(lax.ppermute(half, "tm", along))
-    for plane, quarter in zip((0, 2, 1, PLANES - 1), quarters):
+    for plane, quarter in zip((0, PLANES - 1, 1, PLANES - 1), quarters):
         if plane != PLANES - 1:
             quarter = lax.ppermute(quarter, "tm", [(w, w + 1 - PLANES + plane) for w in last])
         relayed.append(lax.ppermute(quarter, "tm", [(w + 1 - PLANES + plane, w + 1) for w in last]))
     return arrived + relayed
-
-
-def gather_correlation(correlation):
-    own = lax.all_to_all(deal(correlation), "band", 0, 0, tiled=True)
-    far, near = BANDS // 2, 1
-    beside = lax.ppermute(own, "band", [(b, b ^ far) for b in range(BANDS)])
-    across = lax.ppermute(own, "band", [(b, b ^ near) for b in range(BANDS)])
-    return own, beside, across, lax.ppermute(beside, "band", [(b, b ^ near) for b in range(BANDS)])
 
 
 def defects(increments, velocity, diffusivity, scaling, correlation):
@@ -297,9 +255,9 @@
     for base in (0, CH // 2):
         ends.append(propagate(base, x, v, before, after, diffuse, band))
     sent = combine(x, to_next_window(ends), sigma)
-    blocks = gather_correlation(correlation)
+    full = lax.all_gather(correlation, "band", axis=0, tiled=True)
     mine = lax.all_to_all(sent, "band", 0, 0, tiled=True)
-    mixed, hi, lo = mix_rows(quarter_of(band), blocks, mine)
+    mixed, hi, lo = mix_rows(full, mine)
     back = lax.all_to_all(mixed, "band", 0, 0, tiled=True)
     return mix_columns(hi, lo, back, sigma).reshape(1, FIELDS, LEVELS, ROWS, GRID)
 

time: 174 us -> 153 us (0.88)
  blocking collectives: 32.2 us -> 76.1 us
  starting transfers between devices: 58.2 us -> 19.1 us
  waiting for transfers between devices: 55.4 us -> 24.7 us
  between operations: 0.25 us -> 13.6 us
  Pallas kernels: 25.6 us -> 16.9 us
    all_to_all x0 -> x1, blocking collectives: none -> 43.6 us  [defects(): mine = lax.all_to_all(sent, 'band', 0, 0, tiled=True)]
    all_to_all x2 -> x0, starting transfers between devices: 22.3 us -> none  [the longest x1 12.8 us: defects(): mine = lax.all_to_all(sent, 'band', 0, 0, tiled=True)]
    all_to_all x2 -> x0, waiting for transfers between devices: 21.3 us -> none  [the longest x1 21.3 us: defects(): mine = lax.all_to_all(sent, 'band', 0, 0, tiled=True)]
    ppermute x1, waiting for transfers between devices: 18 us -> 0.2 us  [defects(): before = lax.ppermute(hi_edge, 'band', up)]
    ppermute x3 -> x0, starting transfers between devices: 8.99 us -> none  [the longest x1 5.06 us: gather_correlation(): beside = lax.ppermute(own, 'band', [(b, b ^ far) for b in range(BANDS)])]
    ppermute x3 -> x2, waiting for transfers between devices: 5.99 us -> 12 us  [to_next_window(): lax.ppermute(quarter, 'tm', [(w, w + 1 - PLANES + plane) for w in last])]
    ppermute x4, starting transfers between devices: 10.9 us -> 5.96 us  [to_next_window(): lax.ppermute(quarter, 'tm', [(w + 1 - PLANES + plane, w + 1) for w in last])]
    pallas_call x2, Pallas kernels: 10.9 us -> 6.89 us  [propagate(): pl.pallas_call(functools.partial(stencil_kernel, base), out_shape=tuple((...]
  transfers between devices with their start and end apart: 16 -> 11, of which waited for: 6 -> 5; matrix products, arithmetic and copies ran while one was open for 0% -> 1% of each run, Pallas kernels for 9% -> 6%
where the time goes in v3:
time: 153 us; the launch traced here: 152 us
  blocking collectives  76.1 us (50%)
  waiting for transfers between devices  24.7 us (16%)
  starting transfers between devices  19.1 us (12%)
  Pallas kernels  16.9 us (11%)
  between operations  13.6 us (9%)
  local copies, waits for them, and re-layouts  1.81 us (1%)
    all_to_all x1, blocking collectives, defects(): mine = lax.all_to_all(sent, 'band', 0, 0, tiled=True)  43.6 us
    all_to_all x1, blocking collectives, defects(): back = lax.all_to_all(mixed, 'band', 0, 0, tiled=True)  32.5 us
    ppermute x2, waiting for transfers between devices, to_next_window(): lax.ppermute(quarter, 'tm', [(w, w + 1 - PLANES + plane) for w in last])  12 us
    ppermute x4, waiting for transfers between devices, to_next_window(): lax.ppermute(quarter, 'tm', [(w + 1 - PLANES + plane, w + 1) for w in last])  9.99 us
    pallas_call x2, Pallas kernels, propagate(): pl.pallas_call(functools.partial(stencil_kernel, base), out_shape=tuple((...  6.89 us
    ppermute x4, starting transfers between devices, to_next_window(): lax.ppermute(quarter, 'tm', [(w + 1 - PLANES + plane, w + 1) for w in last])  5.96 us
    ppermute x2, starting transfers between devices, to_next_window(): arrived.append(lax.ppermute(half, 'tm', along))  5.6 us
    pallas_call x1, Pallas kernels, mix_rows(): pl.pallas_call(rows_kernel, grid=(GRID // 256,), out_shape=(jax.ShapeDtyp...  4.51 us
  transfers between devices with their start and end apart: 11, of which 5 were waited for; matrix products, arithmetic and copies ran while one was open for 1% of the time, Pallas kernels for 6%

profile of v3, /device:TPU:136, one launch (start us, length us, event | category | flops | bytes accessed | tf_op | source)
XLA Modules:
  0.0 152.2 jit_solution(2758055258304779443)
XLA Ops:
  6.5 0.0 copy-start
  6.5 0.0 all-gather.2.cloned.1.call-start
  6.5 0.7 all-gather.2.cloned.1.call-update
  7.3 0.0 copy-start.1
  7.3 1.2 pack_edges.1
  8.5 1.9 %collective-permute-start = (f32[5,8,1024]{2,1,0:T(8,128)S(1)}, f32[5,8,1024]{2,1,0:T(8,128)S(1)}, u32[]{:S(2)}, u32[]{:S(2)}) collective-permute-start(f32[5,8,1024]{2,1,0:T(8,128)S(1)} %get-tuple-element.16), channel_id=1, source_target_pairs={{0,1},{1,2},{2,3},{3,4},{4,5},{5,6},{6,7},{7,8},{8,9},{9,10},{10,1... | collective-permute-start | bytes 491528 | tf_op jit(solution)/shard_map/ppermute | solution.py:250
  10.4 3.6 %collective-permute-start.1 = (f32[5,8,1024]{2,1,0:T(8,128)S(1)}, f32[5,8,1024]{2,1,0:T(8,128)S(1)}, u32[]{:S(2)}, u32[]{:S(2)}) collective-permute-start(f32[5,8,1024]{2,1,0:T(8,128)S(1)} %get-tuple-element.17), channel_id=1, source_target_pairs={{1,0},{2,1},{3,2},{4,3},{5,4},{6,5},{7,6},{8,7},{9,8},{10,9},{11,1... | collective-permute-start | bytes 491528 | tf_op jit(solution)/shard_map/ppermute | solution.py:251
  14.0 0.8 copy.7
  14.8 0.1 reshape.16.k_ref
  14.9 0.2 collective-permute-done.before_ref
  15.1 1.8 %collective-permute-done.1.after_ref = f32[5,8,1024]{2,1,0:T(8,128)S(1)} collective-permute-done((f32[5,8,1024]{2,1,0:T(8,128)S(1)}, f32[5,8,1024]{2,1,0:T(8,128)S(1)}, u32[]{:S(2)}, u32[]{:S(2)}) %collective-permute-start.1) | collective-permute-done | bytes 163872 | tf_op jit(solution)/shard_map/ppermute | solution.py:251
  16.9 0.0 copy-done
  16.9 0.0 copy-start.2
  16.9 0.9 copy-done.2
  17.8 3.4 %propagate.3 = (f32[4,32,1024]{2,1,0:T(8,128)S(1)}, f32[2,32,1024]{2,1,0:T(8,128)S(1)}, f32[2,32,1024]{2,1,0:T(8,128)S(1)}) custom-call(f32[8]{0:T(128)S(1)} %reshape.16.k_ref, s32[1]{0:T(128)} %bitcast.1.band_ref, f32[8,32,1024]{2,1,0:T(8,128)S(1)} %bitcast.6, f32[2,32,1024]{2,1,0:T(8,128)S(1)} %bitcast.12, ...), custom_call_target="tpu_custom_call" | custom-call | tf_op jit(solution)/shard_map/propagate/pallas_call | solution.py:125
  21.3 0.7 collective-permute-start.7
  21.9 1.3 collective-permute-start.9
  23.2 3.4 %propagate.2 = (f32[4,32,1024]{2,1,0:T(8,128)S(1)}, f32[2,32,1024]{2,1,0:T(8,128)S(1)}, f32[2,32,1024]{2,1,0:T(8,128)S(1)}) custom-call(f32[8]{0:T(128)S(1)} %reshape.16.k_ref, s32[1]{0:T(128)} %bitcast.1.band_ref, f32[8,32,1024]{2,1,0:T(8,128)S(1)} %bitcast.7, f32[2,32,1024]{2,1,0:T(8,128)S(1)} %bitcast.13, ...), custom_call_target="tpu_custom_call" | custom-call | tf_op jit(solution)/shard_map/propagate/pallas_call | solution.py:125
  26.7 1.3 collective-permute-start.4
  28.0 2.8 %collective-permute-start.3 = (f32[4,32,1024]{2,1,0:T(8,128)S(1)}, f32[4,32,1024]{2,1,0:T(8,128)S(1)}, u32[]{:S(2)}, u32[]{:S(2)}) collective-permute-start(f32[4,32,1024]{2,1,0:T(8,128)S(1)} %get-tuple-element.19), channel_id=1, source_target_pairs={{0,32},{32,64},{64,96},{128,160},{160,192},{192,224},{256,288},{28... | collective-permute-start | bytes 1572872 | tf_op jit(solution)/shard_map/ppermute | solution.py:235
  30.8 2.8 %collective-permute-start.2 = (f32[4,32,1024]{2,1,0:T(8,128)S(1)}, f32[4,32,1024]{2,1,0:T(8,128)S(1)}, u32[]{:S(2)}, u32[]{:S(2)}) collective-permute-start(f32[4,32,1024]{2,1,0:T(8,128)S(1)} %get-tuple-element.18), channel_id=1, source_target_pairs={{0,32},{32,64},{64,96},{128,160},{160,192},{192,224},{256,288},{28... | collective-permute-start | bytes 1572872 | tf_op jit(solution)/shard_map/ppermute | solution.py:235
  33.6 0.0 collective-permute-done.7
  33.6 1.3 collective-permute-start.6
  34.9 0.3 collective-permute-done.9.p3
  35.2 1.3 collective-permute-start.8
  36.5 12.0 %collective-permute-done.4 = f32[2,32,1024]{2,1,0:T(8,128)S(1)} collective-permute-done((f32[2,32,1024]{2,1,0:T(8,128)S(1)}, f32[2,32,1024]{2,1,0:T(8,128)S(1)}, u32[]{:S(2)}, u32[]{:S(2)}) %collective-permute-start.4) | collective-permute-done | bytes 262176 | tf_op jit(solution)/shard_map/ppermute | solution.py:238
  48.6 2.1 %collective-permute-start.5 = (f32[2,32,1024]{2,1,0:T(8,128)S(1)}, f32[2,32,1024]{2,1,0:T(8,128)S(1)}, u32[]{:S(2)}, u32[]{:S(2)}) collective-permute-start(f32[2,32,1024]{2,1,0:T(8,128)S(1)} %collective-permute-done.4), channel_id=1, source_target_pairs={{0,128},{128,256},{256,384},{1,129},{129,257},{257,385},{2,130},{1... | collective-permute-start | bytes 786440 | tf_op jit(solution)/shard_map/ppermute | solution.py:239
  50.7 0.0 collective-permute-done.6.p1
  50.7 0.0 collective-permute-done.8.p2
  50.7 0.0 collective-permute-done.3.along1
  50.7 9.7 %collective-permute-done.5.p0 = f32[2,32,1024]{2,1,0:T(8,128)S(1)} collective-permute-done((f32[2,32,1024]{2,1,0:T(8,128)S(1)}, f32[2,32,1024]{2,1,0:T(8,128)S(1)}, u32[]{:S(2)}, u32[]{:S(2)}) %collective-permute-start.5) | collective-permute-done | bytes 262176 | tf_op jit(solution)/shard_map/ppermute | solution.py:239
  60.4 0.0 collective-permute-done.2.along0
  60.4 0.0 copy-done.1
  60.4 1.6 %combine.1 = f32[32,32,256]{2,1,0:T(8,128)S(1)} custom-call(f32[8,32,1024]{2,1,0:T(8,128)S(1)} %bitcast.8, f32[4,32,1024]{2,1,0:T(8,128)S(1)} %collective-permute-done.2.along0, f32[4,32,1024]{2,1,0:T(8,128)S(1)} %collective-permute-done.3.along1, f32[2,32,1024]{2,1,0:T(8,128)S(1)} %collective-permute-done.5.p0, ...), custom_call_target="tpu_custom_call" | custom-call | tf_op jit(solution)/shard_map/combine/pallas_call | solution.py:153
  62.0 43.6 %all_to_all.10.x_ref = f32[32,32,256]{2,1,0:T(8,128)S(1)} all-to-all(f32[32,32,256]{2,1,0:T(8,128)S(1)} %combine.1), channel_id=1, replica_groups=mesh['tm'=16,'band'=32] {'band'}, dimensions={0} | all-to-all | bytes 2097152 | tf_op jit(solution)/shard_map/all_to_all | solution.py:259
  105.6 0.0 all-gather.2.cloned.1.call-done.c_ref
  105.6 4.5 %mix_rows.1 = (f32[32,32,256]{2,1,0:T(8,128)S(1)}, bf16[1024,1024]{1,0:T(8,128)(2,1)S(1)}, bf16[1024,1024]{1,0:T(8,128)(2,1)S(1)}) custom-call(f32[1024,1024]{1,0:T(8,128)} %all-gather.2.cloned.1.call-done.c_ref, f32[32,32,256]{2,1,0:T(8,128)S(1)} %all_to_all.10.x_ref), custom_call_target="tpu_custom_call" | custom-call | tf_op jit(solution)/shard_map/mix_rows/pallas_call | solution.py:183
  110.1 32.5 %all_to_all.11.r_ref = f32[32,32,256]{2,1,0:T(8,128)S(1)} all-to-all(f32[32,32,256]{2,1,0:T(8,128)S(1)} %get-tuple-element.26), channel_id=1, replica_groups=mesh['tm'=16,'band'=32] {'band'}, dimensions={0} | all-to-all | bytes 2097152 | tf_op jit(solution)/shard_map/all_to_all | solution.py:261
  142.6 2.7 %mix_columns.1 = f32[8,32,1024]{2,1,0:T(8,128)} custom-call(bf16[1024,1024]{1,0:T(8,128)(2,1)S(1)} %get-tuple-element.24.hi_ref, bf16[1024,1024]{1,0:T(8,128)(2,1)S(1)} %get-tuple-element.25.lo_ref, f32[32,32,256]{2,1,0:T(8,128)S(1)} %all_to_all.11.r_ref, f32[8,32,1024]{2,1,0:T(8,128)S(1)} %bitcast.10), custom_call_target="tpu_custom_call" | custom-call | tf_op jit(solution)/shard_map/mix_columns/pallas_call | solution.py:216
Async XLA Ops:
  6.5 10.3 %copy-start = (f32[1,4,2,32,1024]{4,3,2,1,0:T(8,128)S(1)}, f32[1,4,2,32,1024]{4,3,2,1,0:T(8,128)}, u32[]{:S(2)}) copy-start(f32[1,4,2,32,1024]{4,3,2,1,0:T(8,128)} %param.5) | copy-start | bytes 3145732
  6.5 99.1 %all-gather.2.cloned.1.call-start = ((), (), s32[]{:S(2)}) async-start(), calls=%async_computation.2 | async-start | bytes 4325376 | tf_op jit(solution)/shard_map/all_gather | solution.py:258
  7.3 53.1 %copy-start.1 = (f32[4,2,32,1024]{3,2,1,0:T(8,128)S(1)}, f32[4,2,32,1024]{3,2,1,0:T(8,128)}, u32[]{:S(2)}) copy-start(f32[4,2,32,1024]{3,2,1,0:T(8,128)} %param.8) | copy-start | bytes 3145732
  8.5 6.6 %collective-permute-start = (f32[5,8,1024]{2,1,0:T(8,128)S(1)}, f32[5,8,1024]{2,1,0:T(8,128)S(1)}, u32[]{:S(2)}, u32[]{:S(2)}) collective-permute-start(f32[5,8,1024]{2,1,0:T(8,128)S(1)} %get-tuple-element.16), channel_id=1, source_target_pairs={{0,1},{1,2},{2,3},{3,4},{4,5},{5,6},{6,7},{7,8},{8,9},{9,10},{10,1... | collective-permute-start | bytes 491528 | tf_op jit(solution)/shard_map/ppermute | solution.py:250
  10.4 6.5 %collective-permute-start.1 = (f32[5,8,1024]{2,1,0:T(8,128)S(1)}, f32[5,8,1024]{2,1,0:T(8,128)S(1)}, u32[]{:S(2)}, u32[]{:S(2)}) collective-permute-start(f32[5,8,1024]{2,1,0:T(8,128)S(1)} %get-tuple-element.17), channel_id=1, source_target_pairs={{1,0},{2,1},{3,2},{4,3},{5,4},{6,5},{7,6},{8,7},{9,8},{10,9},{11,1... | collective-permute-start | bytes 491528 | tf_op jit(solution)/shard_map/ppermute | solution.py:251
  16.9 1.0 copy-start.2
  21.3 12.4 %collective-permute-start.7 = (f32[2,32,1024]{2,1,0:T(8,128)S(1)}, f32[2,32,1024]{2,1,0:T(8,128)S(1)}, u32[]{:S(2)}, u32[]{:S(2)}) collective-permute-start(f32[2,32,1024]{2,1,0:T(8,128)S(1)} %get-tuple-element.22), channel_id=1, source_target_pairs={{96,32},{224,160},{352,288},{97,33},{225,161},{353,289},{98,34},{2... | collective-permute-start | bytes 786440 | tf_op jit(solution)/shard_map/ppermute | solution.py:238
  21.9 13.3 %collective-permute-start.9 = (f32[2,32,1024]{2,1,0:T(8,128)S(1)}, f32[2,32,1024]{2,1,0:T(8,128)S(1)}, u32[]{:S(2)}, u32[]{:S(2)}) collective-permute-start(f32[2,32,1024]{2,1,0:T(8,128)S(1)} %get-tuple-element.23), channel_id=1, source_target_pairs={{96,128},{224,256},{352,384},{97,129},{225,257},{353,385},{98,130}... | collective-permute-start | bytes 786440 | tf_op jit(solution)/shard_map/ppermute | solution.py:239
  26.7 21.9 %collective-permute-start.4 = (f32[2,32,1024]{2,1,0:T(8,128)S(1)}, f32[2,32,1024]{2,1,0:T(8,128)S(1)}, u32[]{:S(2)}, u32[]{:S(2)}) collective-permute-start(f32[2,32,1024]{2,1,0:T(8,128)S(1)} %get-tuple-element.20), channel_id=1, source_target_pairs={{96,0},{224,128},{352,256},{97,1},{225,129},{353,257},{98,2},{226,... | collective-permute-start | bytes 786440 | tf_op jit(solution)/shard_map/ppermute | solution.py:238
  28.0 22.7 %collective-permute-start.3 = (f32[4,32,1024]{2,1,0:T(8,128)S(1)}, f32[4,32,1024]{2,1,0:T(8,128)S(1)}, u32[]{:S(2)}, u32[]{:S(2)}) collective-permute-start(f32[4,32,1024]{2,1,0:T(8,128)S(1)} %get-tuple-element.19), channel_id=1, source_target_pairs={{0,32},{32,64},{64,96},{128,160},{160,192},{192,224},{256,288},{28... | collective-permute-start | bytes 1572872 | tf_op jit(solution)/shard_map/ppermute | solution.py:235
  30.8 29.5 %collective-permute-start.2 = (f32[4,32,1024]{2,1,0:T(8,128)S(1)}, f32[4,32,1024]{2,1,0:T(8,128)S(1)}, u32[]{:S(2)}, u32[]{:S(2)}) collective-permute-start(f32[4,32,1024]{2,1,0:T(8,128)S(1)} %get-tuple-element.18), channel_id=1, source_target_pairs={{0,32},{32,64},{64,96},{128,160},{160,192},{192,224},{256,288},{28... | collective-permute-start | bytes 1572872 | tf_op jit(solution)/shard_map/ppermute | solution.py:235
  33.6 17.0 %collective-permute-start.6 = (f32[2,32,1024]{2,1,0:T(8,128)S(1)}, f32[2,32,1024]{2,1,0:T(8,128)S(1)}, u32[]{:S(2)}, u32[]{:S(2)}) collective-permute-start(f32[2,32,1024]{2,1,0:T(8,128)S(1)} %get-tuple-element.21), channel_id=1, source_target_pairs={{96,128},{224,256},{352,384},{97,129},{225,257},{353,385},{98,130}... | collective-permute-start | bytes 786440 | tf_op jit(solution)/shard_map/ppermute | solution.py:239
  35.2 15.4 %collective-permute-start.8 = (f32[2,32,1024]{2,1,0:T(8,128)S(1)}, f32[2,32,1024]{2,1,0:T(8,128)S(1)}, u32[]{:S(2)}, u32[]{:S(2)}) collective-permute-start(f32[2,32,1024]{2,1,0:T(8,128)S(1)} %collective-permute-done.7), channel_id=1, source_target_pairs={{32,128},{160,256},{288,384},{33,129},{161,257},{289,385},{34,130}... | collective-permute-start | bytes 786440 | tf_op jit(solution)/shard_map/ppermute | solution.py:239
  48.6 11.8 %collective-permute-start.5 = (f32[2,32,1024]{2,1,0:T(8,128)S(1)}, f32[2,32,1024]{2,1,0:T(8,128)S(1)}, u32[]{:S(2)}, u32[]{:S(2)}) collective-permute-start(f32[2,32,1024]{2,1,0:T(8,128)S(1)} %collective-permute-done.4), channel_id=1, source_target_pairs={{0,128},{128,256},{256,384},{1,129},{129,257},{257,385},{2,130},{1... | collective-permute-start | bytes 786440 | tf_op jit(solution)/shard_map/ppermute | solution.py:239
Sparse Core Ops, SparseCore 0:
  9.5 79.2 all-gather.1

commit v4 on v3

--- a/solution.py
+++ b/solution.py
@@ -166,33 +166,32 @@
     return hi, (x - hi.astype(F32)).astype(BF16)
 
 
-def rows_kernel(c_ref, x_ref, o_ref, hi_ref, lo_ref, xh, xl):
+def rows_kernel(c_ref, x_ref, o_ref, xh, xl):
     @pl.when(pl.program_id(0) == 0)
     def _():
         xh[...], xl[...] = halves(x_ref[...].reshape(GRID, COLS))
 
-    hi_ref[...], lo_ref[...] = halves(c_ref[...])
+    hi, lo = halves(c_ref[...])
     dot = lambda a, b: jnp.dot(a, b, preferred_element_type=F32)
-    y = dot(hi_ref[...], xl[...]) + dot(lo_ref[...], xh[...]) + dot(hi_ref[...], xh[...])
+    y = dot(hi, xl[...]) + dot(lo, xh[...]) + dot(hi, xh[...])
     o_ref[...] = y.reshape(8, ROWS, COLS)
 
 
 def mix_rows(c, x):
     whole = pl.BlockSpec((256, GRID), lambda i: (i, 0))
-    shape = jax.ShapeDtypeStruct((GRID, GRID), BF16)
     return pl.pallas_call(
         rows_kernel,
         grid=(GRID // 256,),
-        out_shape=(jax.ShapeDtypeStruct((BANDS, ROWS, COLS), F32), shape, shape),
+        out_shape=jax.ShapeDtypeStruct((BANDS, ROWS, COLS), F32),
         in_specs=[whole, pl.BlockSpec((BANDS, ROWS, COLS), lambda i: (0, 0, 0))],
-        out_specs=(pl.BlockSpec((8, ROWS, COLS), lambda i: (i, 0, 0)), whole, whole),
+        out_specs=pl.BlockSpec((8, ROWS, COLS), lambda i: (i, 0, 0)),
         scratch_shapes=[pltpu.VMEM((GRID, COLS), BF16)] * 2,
         compiler_params=params(12),
         name="mix_rows",
     )(*in_hbm(c), x)
 
 
-def columns_kernel(hi_ref, lo_ref, r_ref, s_ref, o_hbm, rh, rl, buf, sem):
+def columns_kernel(c_ref, r_ref, s_ref, o_hbm, rh, rl, buf, sem):
     for c in range(CH):
         for q in range(QUARTERS):
             at = slice(c * ROWS, (c + 1) * ROWS), slice(q * COLS, (q + 1) * COLS)
@@ -203,7 +202,7 @@
     copies = []
     for i in range(GRID // 256):
         at = slice(i * 256, (i + 1) * 256)
-        hi, lo = hi_ref[at], lo_ref[at]
+        hi, lo = halves(c_ref[at])
         y = dot(rl[...], hi) + dot(rh[...], lo) + dot(rh[...], hi)
         buf[:, :, at] = s_ref[:, :, at] * y.reshape(CH, ROWS, 256)
         copies.append(pltpu.make_async_copy(buf.at[:, :, at], o_hbm.at[:, :, at], sem.at[i]))
@@ -212,17 +211,17 @@
         copy.wait()
 
 
-def mix_columns(hi, lo, r, sigma):
+def mix_columns(c, r, sigma):
     return pl.pallas_call(
         columns_kernel,
         out_shape=jax.ShapeDtypeStruct((CH, ROWS, GRID), F32),
-        in_specs=[VMEM] * 4,
+        in_specs=[VMEM] * 3,
         out_specs=HBM,
         scratch_shapes=[pltpu.VMEM((CH * ROWS, GRID), BF16)] * 2
         + [pltpu.VMEM((CH, ROWS, GRID), F32), pltpu.SemaphoreType.DMA((GRID // 256,))],
-        compiler_params=params(5),
+        compiler_params=params(8),
         name="mix_columns",
-    )(hi, lo, r, sigma)
+    )(c, r, sigma)
 
 
 def to_next_window(ends):
@@ -257,9 +256,9 @@
     sent = combine(x, to_next_window(ends), sigma)
     full = lax.all_gather(correlation, "band", axis=0, tiled=True)
     mine = lax.all_to_all(sent, "band", 0, 0, tiled=True)
-    mixed, hi, lo = mix_rows(full, mine)
+    mixed = mix_rows(full, mine)
     back = lax.all_to_all(mixed, "band", 0, 0, tiled=True)
-    return mix_columns(hi, lo, back, sigma).reshape(1, FIELDS, LEVELS, ROWS, GRID)
+    return mix_columns(full, back, sigma).reshape(1, FIELDS, LEVELS, ROWS, GRID)
 
 
 def solution(mesh):

time: 153 us -> 154 us (level)
  the two profiles are of different devices: /device:TPU:136 before, /device:TPU:8 now
where the time goes in v4:
time: 154 us
  blocking collectives  74.6 us (48%)
  starting transfers between devices  28.7 us (19%)
  Pallas kernels  16.9 us (11%)
  waiting for transfers between devices  15.8 us (10%)
  between operations  13.6 us (9%)
  local copies, waits for them, and re-layouts  4.29 us (3%)
    all_to_all x1, blocking collectives, defects(): mine = lax.all_to_all(sent, 'band', 0, 0, tiled=True)  42.1 us
    all_to_all x1, blocking collectives, defects(): back = lax.all_to_all(mixed, 'band', 0, 0, tiled=True)  32.5 us
    ppermute x4, starting transfers between devices, to_next_window(): lax.ppermute(quarter, 'tm', [(w + 1 - PLANES + plane, w + 1) for w in last])  14.9 us
    pallas_call x2, Pallas kernels, propagate(): pl.pallas_call(functools.partial(stencil_kernel, base), out_shape=tuple((...  6.89 us
    ppermute x2, waiting for transfers between devices, to_next_window(): lax.ppermute(quarter, 'tm', [(w, w + 1 - PLANES + plane) for w in last])  6.73 us
    ppermute x4, waiting for transfers between devices, to_next_window(): lax.ppermute(quarter, 'tm', [(w + 1 - PLANES + plane, w + 1) for w in last])  6.42 us
    ppermute x2, starting transfers between devices, to_next_window(): arrived.append(lax.ppermute(half, 'tm', along))  6.21 us
    pallas_call x1, Pallas kernels, mix_rows(): pl.pallas_call(rows_kernel, grid=(GRID // 256,), out_shape=jax.ShapeDtype...  4.59 us
  transfers between devices with their start and end apart: 11, of which 4 were waited for; matrix products, arithmetic and copies ran while one was open for 1% of the time, Pallas kernels for 6%

profile of v4, /device:TPU:8, one launch (start us, length us, event | category | flops | bytes accessed | tf_op | source)
XLA Modules:
  0.0 153.9 jit_solution(4681848199950501575)
XLA Ops:
  6.5 0.0 copy-start.2
  6.5 0.0 all-gather.2.cloned.1.call-start
  6.5 0.7 all-gather.2.cloned.1.call-update
  7.3 1.1 pack_edges.1
  8.4 1.9 %collective-permute-start = (f32[5,8,1024]{2,1,0:T(8,128)S(1)}, f32[5,8,1024]{2,1,0:T(8,128)S(1)}, u32[]{:S(2)}, u32[]{:S(2)}) collective-permute-start(f32[5,8,1024]{2,1,0:T(8,128)S(1)} %get-tuple-element.13), channel_id=1, source_target_pairs={{0,1},{1,2},{2,3},{3,4},{4,5},{5,6},{6,7},{7,8},{8,9},{9,10},{10,1... | collective-permute-start | bytes 491528 | tf_op jit(solution)/shard_map/ppermute | solution.py:249
  10.3 3.6 %collective-permute-start.1 = (f32[5,8,1024]{2,1,0:T(8,128)S(1)}, f32[5,8,1024]{2,1,0:T(8,128)S(1)}, u32[]{:S(2)}, u32[]{:S(2)}) collective-permute-start(f32[5,8,1024]{2,1,0:T(8,128)S(1)} %get-tuple-element.14), channel_id=1, source_target_pairs={{1,0},{2,1},{3,2},{4,3},{5,4},{6,5},{7,6},{8,7},{9,8},{10,9},{11,1... | collective-permute-start | bytes 491528 | tf_op jit(solution)/shard_map/ppermute | solution.py:250
  14.0 0.8 copy.7
  14.7 0.1 reshape.16.k_ref
  14.8 0.2 collective-permute-done.before_ref
  15.0 1.8 %collective-permute-done.1.after_ref = f32[5,8,1024]{2,1,0:T(8,128)S(1)} collective-permute-done((f32[5,8,1024]{2,1,0:T(8,128)S(1)}, f32[5,8,1024]{2,1,0:T(8,128)S(1)}, u32[]{:S(2)}, u32[]{:S(2)}) %collective-permute-start.1) | collective-permute-done | bytes 163872 | tf_op jit(solution)/shard_map/ppermute | solution.py:250
  16.8 0.0 copy-start.1
  16.8 1.2 copy-done.1
  18.0 0.0 copy-start.5
  18.0 0.9 copy-done.5
  18.9 3.4 %propagate.3 = (f32[4,32,1024]{2,1,0:T(8,128)S(1)}, f32[2,32,1024]{2,1,0:T(8,128)S(1)}, f32[2,32,1024]{2,1,0:T(8,128)S(1)}) custom-call(f32[8]{0:T(128)S(1)} %reshape.16.k_ref, s32[1]{0:T(128)} %bitcast.1.band_ref, f32[8,32,1024]{2,1,0:T(8,128)S(1)} %bitcast.6, f32[2,32,1024]{2,1,0:T(8,128)S(1)} %bitcast.12, ...), custom_call_target="tpu_custom_call" | custom-call | tf_op jit(solution)/shard_map/propagate/pallas_call | solution.py:125
  22.4 0.7 collective-permute-start.7
  23.1 0.7 collective-permute-start.9
  23.8 3.4 %propagate.2 = (f32[4,32,1024]{2,1,0:T(8,128)S(1)}, f32[2,32,1024]{2,1,0:T(8,128)S(1)}, f32[2,32,1024]{2,1,0:T(8,128)S(1)}) custom-call(f32[8]{0:T(128)S(1)} %reshape.16.k_ref, s32[1]{0:T(128)} %bitcast.1.band_ref, f32[8,32,1024]{2,1,0:T(8,128)S(1)} %bitcast.7, f32[2,32,1024]{2,1,0:T(8,128)S(1)} %bitcast.13, ...), custom_call_target="tpu_custom_call" | custom-call | tf_op jit(solution)/shard_map/propagate/pallas_call | solution.py:125
  27.2 1.3 collective-permute-start.4
  28.5 3.4 %collective-permute-start.3 = (f32[4,32,1024]{2,1,0:T(8,128)S(1)}, f32[4,32,1024]{2,1,0:T(8,128)S(1)}, u32[]{:S(2)}, u32[]{:S(2)}) collective-permute-start(f32[4,32,1024]{2,1,0:T(8,128)S(1)} %get-tuple-element.16), channel_id=1, source_target_pairs={{0,32},{32,64},{64,96},{128,160},{160,192},{192,224},{256,288},{28... | collective-permute-start | bytes 1572872 | tf_op jit(solution)/shard_map/ppermute | solution.py:234
  31.9 2.8 %collective-permute-start.2 = (f32[4,32,1024]{2,1,0:T(8,128)S(1)}, f32[4,32,1024]{2,1,0:T(8,128)S(1)}, u32[]{:S(2)}, u32[]{:S(2)}) collective-permute-start(f32[4,32,1024]{2,1,0:T(8,128)S(1)} %get-tuple-element.15), channel_id=1, source_target_pairs={{0,32},{32,64},{64,96},{128,160},{160,192},{192,224},{256,288},{28... | collective-permute-start | bytes 1572872 | tf_op jit(solution)/shard_map/ppermute | solution.py:234
  34.7 0.0 collective-permute-done.7
  34.8 0.7 collective-permute-start.6
  35.4 0.0 collective-permute-done.9.p3
  35.4 0.7 collective-permute-start.8
  36.1 6.7 %collective-permute-done.4 = f32[2,32,1024]{2,1,0:T(8,128)S(1)} collective-permute-done((f32[2,32,1024]{2,1,0:T(8,128)S(1)}, f32[2,32,1024]{2,1,0:T(8,128)S(1)}, u32[]{:S(2)}, u32[]{:S(2)}) %collective-permute-start.4) | collective-permute-done | bytes 262176 | tf_op jit(solution)/shard_map/ppermute | solution.py:237
  42.9 12.9 %collective-permute-start.5 = (f32[2,32,1024]{2,1,0:T(8,128)S(1)}, f32[2,32,1024]{2,1,0:T(8,128)S(1)}, u32[]{:S(2)}, u32[]{:S(2)}) collective-permute-start(f32[2,32,1024]{2,1,0:T(8,128)S(1)} %collective-permute-done.4), channel_id=1, source_target_pairs={{0,128},{128,256},{256,384},{1,129},{129,257},{257,385},{2,130},{1... | collective-permute-start | bytes 786440 | tf_op jit(solution)/shard_map/ppermute | solution.py:238
  55.8 0.0 collective-permute-done.6.p1
  55.8 0.0 collective-permute-done.8.p2
  55.8 0.0 collective-permute-done.3.along1
  55.8 6.4 %collective-permute-done.5.p0 = f32[2,32,1024]{2,1,0:T(8,128)S(1)} collective-permute-done((f32[2,32,1024]{2,1,0:T(8,128)S(1)}, f32[2,32,1024]{2,1,0:T(8,128)S(1)}, u32[]{:S(2)}, u32[]{:S(2)}) %collective-permute-start.5) | collective-permute-done | bytes 262176 | tf_op jit(solution)/shard_map/ppermute | solution.py:238
  62.2 0.0 collective-permute-done.2.along0
  62.2 0.0 copy-done.2
  62.2 0.0 copy-start.3
  62.2 1.2 copy-done.3
  63.5 1.6 %combine.1 = f32[32,32,256]{2,1,0:T(8,128)S(1)} custom-call(f32[8,32,1024]{2,1,0:T(8,128)S(1)} %bitcast.8, f32[4,32,1024]{2,1,0:T(8,128)S(1)} %collective-permute-done.2.along0, f32[4,32,1024]{2,1,0:T(8,128)S(1)} %collective-permute-done.3.along1, f32[2,32,1024]{2,1,0:T(8,128)S(1)} %collective-permute-done.5.p0, ...), custom_call_target="tpu_custom_call" | custom-call | tf_op jit(solution)/shard_map/combine/pallas_call | solution.py:153
  65.1 42.1 %all_to_all.10.x_ref = f32[32,32,256]{2,1,0:T(8,128)S(1)} all-to-all(f32[32,32,256]{2,1,0:T(8,128)S(1)} %combine.1), channel_id=1, replica_groups=mesh['tm'=16,'band'=32] {'band'}, dimensions={0} | all-to-all | bytes 2097152 | tf_op jit(solution)/shard_map/all_to_all | solution.py:258
  107.2 0.0 copy-start.4
  107.2 0.0 all-gather.2.cloned.1.call-done.c_ref
  107.2 0.0 copy-start
  107.2 4.6 %mix_rows.1 = f32[32,32,256]{2,1,0:T(8,128)S(1)} custom-call(f32[1024,1024]{1,0:T(8,128)} %all-gather.2.cloned.1.call-done.c_ref, f32[32,32,256]{2,1,0:T(8,128)S(1)} %all_to_all.10.x_ref), custom_call_target="tpu_custom_call" | custom-call | tf_op jit(solution)/shard_map/mix_rows/pallas_call | solution.py:182
  111.8 32.5 %all_to_all.11.r_ref = f32[32,32,256]{2,1,0:T(8,128)S(1)} all-to-all(f32[32,32,256]{2,1,0:T(8,128)S(1)} %mix_rows.1), channel_id=1, replica_groups=mesh['tm'=16,'band'=32] {'band'}, dimensions={0} | all-to-all | bytes 2097152 | tf_op jit(solution)/shard_map/all_to_all | solution.py:260
  144.3 0.0 copy-done.4
  144.3 0.0 copy-done
  144.3 2.7 %mix_columns.1 = f32[8,32,1024]{2,1,0:T(8,128)} custom-call(f32[1024,1024]{1,0:T(8,128)S(1)} %copy-done, f32[32,32,256]{2,1,0:T(8,128)S(1)} %all_to_all.11.r_ref, f32[8,32,1024]{2,1,0:T(8,128)S(1)} %bitcast.10), custom_call_target="tpu_custom_call" | custom-call | tf_op jit(solution)/shard_map/mix_columns/pallas_call | solution.py:215
Async XLA Ops:
  6.5 55.7 %copy-start.2 = (f32[1,4,2,32,1024]{4,3,2,1,0:T(8,128)S(1)}, f32[1,4,2,32,1024]{4,3,2,1,0:T(8,128)}, u32[]{:S(2)}) copy-start(f32[1,4,2,32,1024]{4,3,2,1,0:T(8,128)} %param.5) | copy-start | bytes 3145732
  6.5 100.7 %all-gather.2.cloned.1.call-start = ((), (), s32[]{:S(2)}) async-start(), calls=%async_computation.2 | async-start | bytes 4325376 | tf_op jit(solution)/shard_map/all_gather | solution.py:257
  8.4 6.6 %collective-permute-start = (f32[5,8,1024]{2,1,0:T(8,128)S(1)}, f32[5,8,1024]{2,1,0:T(8,128)S(1)}, u32[]{:S(2)}, u32[]{:S(2)}) collective-permute-start(f32[5,8,1024]{2,1,0:T(8,128)S(1)} %get-tuple-element.13), channel_id=1, source_target_pairs={{0,1},{1,2},{2,3},{3,4},{4,5},{5,6},{6,7},{7,8},{8,9},{9,10},{10,1... | collective-permute-start | bytes 491528 | tf_op jit(solution)/shard_map/ppermute | solution.py:249
  10.3 6.5 %collective-permute-start.1 = (f32[5,8,1024]{2,1,0:T(8,128)S(1)}, f32[5,8,1024]{2,1,0:T(8,128)S(1)}, u32[]{:S(2)}, u32[]{:S(2)}) collective-permute-start(f32[5,8,1024]{2,1,0:T(8,128)S(1)} %get-tuple-element.14), channel_id=1, source_target_pairs={{1,0},{2,1},{3,2},{4,3},{5,4},{6,5},{7,6},{8,7},{9,8},{10,9},{11,1... | collective-permute-start | bytes 491528 | tf_op jit(solution)/shard_map/ppermute | solution.py:250
  16.8 1.2 copy-start.1
  18.0 0.9 copy-start.5
  22.4 12.4 %collective-permute-start.7 = (f32[2,32,1024]{2,1,0:T(8,128)S(1)}, f32[2,32,1024]{2,1,0:T(8,128)S(1)}, u32[]{:S(2)}, u32[]{:S(2)}) collective-permute-start(f32[2,32,1024]{2,1,0:T(8,128)S(1)} %get-tuple-element.19), channel_id=1, source_target_pairs={{96,32},{224,160},{352,288},{97,33},{225,161},{353,289},{98,34},{2... | collective-permute-start | bytes 786440 | tf_op jit(solution)/shard_map/ppermute | solution.py:237
  23.1 12.4 %collective-permute-start.9 = (f32[2,32,1024]{2,1,0:T(8,128)S(1)}, f32[2,32,1024]{2,1,0:T(8,128)S(1)}, u32[]{:S(2)}, u32[]{:S(2)}) collective-permute-start(f32[2,32,1024]{2,1,0:T(8,128)S(1)} %get-tuple-element.20), channel_id=1, source_target_pairs={{96,128},{224,256},{352,384},{97,129},{225,257},{353,385},{98,130}... | collective-permute-start | bytes 786440 | tf_op jit(solution)/shard_map/ppermute | solution.py:238
  27.2 15.6 %collective-permute-start.4 = (f32[2,32,1024]{2,1,0:T(8,128)S(1)}, f32[2,32,1024]{2,1,0:T(8,128)S(1)}, u32[]{:S(2)}, u32[]{:S(2)}) collective-permute-start(f32[2,32,1024]{2,1,0:T(8,128)S(1)} %get-tuple-element.17), channel_id=1, source_target_pairs={{96,0},{224,128},{352,256},{97,1},{225,129},{353,257},{98,2},{226,... | collective-permute-start | bytes 786440 | tf_op jit(solution)/shard_map/ppermute | solution.py:237
  28.5 27.3 %collective-permute-start.3 = (f32[4,32,1024]{2,1,0:T(8,128)S(1)}, f32[4,32,1024]{2,1,0:T(8,128)S(1)}, u32[]{:S(2)}, u32[]{:S(2)}) collective-permute-start(f32[4,32,1024]{2,1,0:T(8,128)S(1)} %get-tuple-element.16), channel_id=1, source_target_pairs={{0,32},{32,64},{64,96},{128,160},{160,192},{192,224},{256,288},{28... | collective-permute-start | bytes 1572872 | tf_op jit(solution)/shard_map/ppermute | solution.py:234
  31.9 30.3 %collective-permute-start.2 = (f32[4,32,1024]{2,1,0:T(8,128)S(1)}, f32[4,32,1024]{2,1,0:T(8,128)S(1)}, u32[]{:S(2)}, u32[]{:S(2)}) collective-permute-start(f32[4,32,1024]{2,1,0:T(8,128)S(1)} %get-tuple-element.15), channel_id=1, source_target_pairs={{0,32},{32,64},{64,96},{128,160},{160,192},{192,224},{256,288},{28... | collective-permute-start | bytes 1572872 | tf_op jit(solution)/shard_map/ppermute | solution.py:234
  34.8 21.0 %collective-permute-start.6 = (f32[2,32,1024]{2,1,0:T(8,128)S(1)}, f32[2,32,1024]{2,1,0:T(8,128)S(1)}, u32[]{:S(2)}, u32[]{:S(2)}) collective-permute-start(f32[2,32,1024]{2,1,0:T(8,128)S(1)} %get-tuple-element.18), channel_id=1, source_target_pairs={{96,128},{224,256},{352,384},{97,129},{225,257},{353,385},{98,130}... | collective-permute-start | bytes 786440 | tf_op jit(solution)/shard_map/ppermute | solution.py:238
  35.4 20.4 %collective-permute-start.8 = (f32[2,32,1024]{2,1,0:T(8,128)S(1)}, f32[2,32,1024]{2,1,0:T(8,128)S(1)}, u32[]{:S(2)}, u32[]{:S(2)}) collective-permute-start(f32[2,32,1024]{2,1,0:T(8,128)S(1)} %collective-permute-done.7), channel_id=1, source_target_pairs={{32,128},{160,256},{288,384},{33,129},{161,257},{289,385},{34,130}... | collective-permute-start | bytes 786440 | tf_op jit(solution)/shard_map/ppermute | solution.py:238
  42.9 19.4 %collective-permute-start.5 = (f32[2,32,1024]{2,1,0:T(8,128)S(1)}, f32[2,32,1024]{2,1,0:T(8,128)S(1)}, u32[]{:S(2)}, u32[]{:S(2)}) collective-permute-start(f32[2,32,1024]{2,1,0:T(8,128)S(1)} %collective-permute-done.4), channel_id=1, source_target_pairs={{0,128},{128,256},{256,384},{1,129},{129,257},{257,385},{2,130},{1... | collective-permute-start | bytes 786440 | tf_op jit(solution)/shard_map/ppermute | solution.py:238
  62.2 1.2 copy-start.3
  107.2 37.1 %copy-start.4 = (f32[4,2,32,1024]{3,2,1,0:T(8,128)S(1)}, f32[4,2,32,1024]{3,2,1,0:T(8,128)}, u32[]{:S(2)}) copy-start(f32[4,2,32,1024]{3,2,1,0:T(8,128)} %param.8) | copy-start | bytes 3145732
  107.2 37.1 %copy-start = (f32[1024,1024]{1,0:T(8,128)S(1)}, f32[1024,1024]{1,0:T(8,128)}, u32[]{:S(2)}) copy-start(f32[1024,1024]{1,0:T(8,128)} %all-gather.2.cloned.1.call-done.c_ref) | copy-start | bytes 12582916
Sparse Core Ops, SparseCore 0:
  9.5 73.1 all-gather.1
